TPU v7x, 768 devices: a whole 4x8x12 slice. The times are simulated.
768 devices in a mesh: tile: 128 (over y, z_lo, x), lev: 6 (over z_hi, core).
Axes of the slice: x: 4, y: 8, z: 12 (z_hi: 3, z_lo: 4; z = z_hi * 4 + z_lo), core: 2. Of those that a mesh axis runs over, the one named last changes fastest.
Arguments:
- sources: float32 [2, 6, 384, 1024], P(None, 'lev', 'tile'), may hold values from -60 to 60
- mass_coef: float32 [384, 1024], P('tile'), may hold values from 0.0005 to 0.002
- neighbour_sub: int32 [384, 4], replicated, may hold values from 0 to 383, as said below
- neighbour_side: int32 [384, 4], replicated, may hold values from 0 to 3
- side_flip: int32 [384, 4], replicated, may hold values from 0 to 1
Outputs:
- solution: float32 [2, 6, 384, 1024], P(None, 'lev', 'tile')
- residual: float32 [2, 6, 384, 1024], P(None, 'lev', 'tile')
Inputs may be any that keep to these rules, and one draw needn't show every extreme that they name: `neighbour_sub`: the sides pair up as the sides of the subdomains on the six faces of a cube, 8 x 8 subdomains a face, with the subdomains numbered and oriented arbitrarily; a side's neighbour lists it back.
All inputs are finite; a program needn't handle non-finite values.
Results may differ from a plain program's by a relative error of at most 0.0003.
Values sent between devices are 32-bit elements; how exact they have to be, the bound alone decides.
A program may use at most 32 MiB of HBM per device.

v0:
```python
import math

import jax
import jax.numpy as jnp
from jax import lax
from jax.sharding import Mesh
from jax.sharding import PartitionSpec as P

ITERS = 2
TILE = ("tile_0", "tile_1", "tile_2")
TILE_LEV = ("tile_0", "tile_1", "tile_2", "lev_0", "lev_1")
LEV = ("lev_0", "lev_1")


HIGH = lax.Precision.HIGHEST


def joined_along(tiles, dim):
    lengths = list(tiles.shape[1:])
    lengths[dim] *= tiles.shape[0]
    return jnp.moveaxis(tiles, 0, dim).reshape(lengths)


def gather_in_order(x, axes, order):
    tiles = x[None]
    for k in order:
        tiles = lax.all_gather(tiles, axes[k], axis=0, tiled=True)
    current = [lax.axis_size(axes[k]) for k in reversed(order)]
    tiles = tiles.reshape(*current, *x.shape)
    turned = sorted(range(len(order)), key=lambda place: order[len(order) - 1 - place])
    return tiles.transpose(*turned, *range(len(order), tiles.ndim)).reshape(-1, *x.shape)


def whole_of(x, axes, order, dim):
    return joined_along(gather_in_order(x, axes, order), dim)


def side_by_side(arrays, axis, dim, along):
    widths = [math.prod(a.shape[along:]) for a in arrays]
    both = jnp.concatenate(
        [a.reshape(*a.shape[:along], w) for a, w in zip(arrays, widths)], axis=along
    )
    result = lax.all_gather(both, axis, axis=dim, tiled=True)
    tiles = jnp.split(result, [sum(widths[:k]) for k in range(1, len(widths))], axis=along)
    return tuple(
        (b.reshape(*result.shape[:along], *a.shape[along:]) for a, b in zip(arrays, tiles))
    )


def over_axes(x, axes):
    for axis in axes:
        x = lax.psum(x, axis)
    return x


def sine_table(edge_len):
    ordinal = jnp.arange(edge_len, dtype=jnp.float32) + 1.0
    step_angle = math.pi / (edge_len + 1.0)
    sine_rows = math.sqrt(2.0 / (edge_len + 1.0)) * jnp.sin(
        step_angle * ordinal[:, None] * ordinal[None, :]
    )
    spectrum = 2.0 - 2.0 * jnp.cos(step_angle * ordinal)
    return (sine_rows, spectrum)


def local_solve(vector, edge_len):
    sine_rows, spectrum = sine_table(edge_len)
    divisor = spectrum[:, None] + spectrum[None, :]
    spectral = jnp.einsum("ij,abnjk->abnik", sine_rows, vector, precision=HIGH)
    spectral = jnp.einsum("abnik,kl->abnil", spectral, sine_rows, precision=HIGH)
    spectral = spectral / divisor
    restored = jnp.einsum("ij,abnjk->abnik", sine_rows, spectral, precision=HIGH)
    return jnp.einsum("abnik,kl->abnil", restored, sine_rows, precision=HIGH)


def field_rims(vector):
    return jnp.stack(
        [vector[..., 0, :], vector[..., :, -1], vector[..., -1, :], vector[..., :, 0]], axis=-2
    )


def operate(vector, mass_grid, received):
    padded = jnp.pad(vector, ((0, 0), (0, 0), (0, 0), (1, 1), (1, 1)))
    beside = (
        padded[..., 2:, 1:-1]
        + padded[..., :-2, 1:-1]
        + padded[..., 1:-1, 2:]
        + padded[..., 1:-1, :-2]
    )
    beside = beside.at[..., 0, :].add(received[..., 0, :])
    beside = beside.at[..., :, -1].add(received[..., 1, :])
    beside = beside.at[..., -1, :].add(received[..., 2, :])
    beside = beside.at[..., :, 0].add(received[..., 3, :])
    return (4.0 + mass_grid) * vector - beside


def coarse_factor(mass_sums, neighbour_sub, edge_len):
    count_all = mass_sums.shape[0]
    sub_ids = jnp.arange(count_all, dtype=jnp.int32)
    adjacency = jnp.sum(
        (neighbour_sub[:, :, None] == sub_ids[None, None, :]).astype(jnp.float32), axis=1
    )
    matrix = edge_len * (4.0 * jnp.eye(count_all, dtype=jnp.float32) - adjacency) + jnp.diag(
        mass_sums
    )
    return jnp.linalg.cholesky(matrix)


def coarse_solve(factor, sums):
    count_all = factor.shape[0]
    columns = sums.reshape(-1, count_all).T
    middle = lax.linalg.triangular_solve(
        factor, columns, left_side=True, lower=True, transpose_a=False
    )
    solved = lax.linalg.triangular_solve(
        factor, middle, left_side=True, lower=True, transpose_a=True
    )
    return solved.T.reshape(sums.shape)


def spread(scalars):
    return scalars[:, None, None, None, None]


def dot_local(left, right):
    return jnp.sum(left * right, axis=(1, 2, 3, 4))


def shards(sources, mass_coef, neighbour_sub, neighbour_side, side_flip):
    edge_len = math.isqrt(sources.shape[-1])
    sub_dev = sources.shape[2]
    lev_dev = sources.shape[1]
    subs_all = sub_dev * lax.axis_size(TILE)
    grid_shape = (2, lev_dev, sub_dev, edge_len, edge_len)
    first_sub = lax.axis_index(TILE) * sub_dev
    my_nbr = lax.dynamic_slice_in_dim(neighbour_sub, first_sub, sub_dev, 0)
    my_side = lax.dynamic_slice_in_dim(neighbour_side, first_sub, sub_dev, 0)
    my_flip = lax.dynamic_slice_in_dim(side_flip, first_sub, sub_dev, 0)
    wanted = (my_nbr * 4 + my_side).reshape(-1)
    flipped = (my_flip.reshape(-1) == 1)[:, None]
    sub_ids = jnp.arange(subs_all, dtype=jnp.int32)
    nbr_select = (my_nbr.reshape(-1)[:, None] == sub_ids[None, :]).astype(jnp.float32)
    mass_grid = mass_coef.reshape(sub_dev, edge_len, edge_len)
    mass_all = whole_of(jnp.sum(mass_coef, axis=-1), TILE, (1, 0, 2), 0)
    factor = coarse_factor(mass_all, neighbour_sub, edge_len)

    def pick(piece):
        piece_subs = piece.shape[2]
        slot_ids = jnp.arange(piece_subs * 4, dtype=jnp.int32)
        selector = (wanted[:, None] == slot_ids[None, :]).astype(jnp.float32)
        flat_rims = piece.reshape(2, lev_dev, piece_subs * 4, edge_len)
        return jnp.einsum("cq,abqs->abcs", selector, flat_rims, precision=HIGH)

    def orient(gotten):
        turned = jnp.where(flipped, gotten[..., ::-1], gotten)
        return turned.reshape(2, lev_dev, sub_dev, 4, edge_len)

    def outgoing(vector):
        return field_rims(vector).reshape(2, lev_dev, sub_dev, 4 * edge_len)

    def mine_of(coarse):
        return lax.dynamic_slice_in_dim(coarse, first_sub, sub_dev, 2)

    def precondition(vector):
        local_part = local_solve(vector, edge_len)
        sums = jnp.sum(vector, axis=(3, 4))
        pieces = side_by_side((outgoing(local_part), sums), TILE, 2, 3)
        gotten = pick(pieces[0])
        all_sums = pieces[1]
        coarse = coarse_solve(factor, all_sums)
        beyond = jnp.einsum("cq,abq->abc", nbr_select, coarse, precision=HIGH)
        rims = orient(gotten) + beyond.reshape(2, lev_dev, sub_dev, 4)[..., None]
        return (local_part + mine_of(coarse)[..., None, None], rims)

    def pair_sums(resid_now, corr_now, image_now):
        return (
            over_axes(dot_local(resid_now, corr_now), TILE_LEV),
            over_axes(dot_local(corr_now, image_now), TILE_LEV),
        )

    residual = sources.reshape(grid_shape)
    solution = jnp.zeros(grid_shape, jnp.float32)
    corrected, rims_z = precondition(residual)
    image = operate(corrected, mass_grid, rims_z)
    gamma_sum, delta_sum = pair_sums(residual, corrected, image)
    step_size = gamma_sum / delta_sum
    direction, along_dir = (corrected, image)
    for step in range(ITERS):
        solution = solution + spread(step_size) * direction
        residual = residual - spread(step_size) * along_dir
        if step + 1 < ITERS:
            corrected, rims_z = precondition(residual)
            image = operate(corrected, mass_grid, rims_z)
            gamma_next, delta_next = pair_sums(residual, corrected, image)
            beta_coef = gamma_next / gamma_sum
            step_size = gamma_next / (delta_next - beta_coef * gamma_next / step_size)
            direction = corrected + spread(beta_coef) * direction
            along_dir = image + spread(beta_coef) * along_dir
            gamma_sum = gamma_next
    out_shape = sources.shape
    return (solution.reshape(out_shape), residual.reshape(out_shape))


def solution(mesh):
    split = Mesh(
        mesh.devices.reshape(8, 4, 4, 3, 2), ("tile_0", "tile_1", "tile_2", "lev_0", "lev_1")
    )
    placed = (P(None, LEV, TILE, None), P(TILE, None), P(), P(), P())
    return jax.shard_map(
        shards,
        mesh=split,
        in_specs=placed,
        out_specs=(P(None, LEV, TILE, None), P(None, LEV, TILE, None)),
        check_vma=False,
    )
```

profile of v0, /device:TPU:1, one launch (start us, length us, event | category | flops | bytes accessed | tf_op | source)
XLA Modules:
  0.0 991.2 jit_solution(4812280544569299481)
XLA Ops:
  0.6 1.3 dynamic-slice.76
  2.6 0.8 broadcast_add_fusion
  3.7 13.1 %all-reduce.3 = f32[12]{0:T(128)S(1)} all-reduce(f32[12]{0:T(128)S(1)} %dynamic-update-slice.45), channel_id=2, replica_groups=mesh['tile_0'=8,'tile_1'=4,'tile_2'=4,'lev_0'=3,'lev_1'=2] {'tile_1'}, use_global_device_ids=true, to_apply=%add.3 | all-reduce | flops 12 | bytes 96
  16.9 18.3 %all-gather.1 = f32[8,4,3]{2,1,0:T(4,128)S(1)} all-gather(f32[1,4,3]{2,1,0:T(4,128)S(1)} %reshape.673), channel_id=1, replica_groups=mesh['tile_0'=8,'tile_1'=4,'tile_2'=4,'lev_0'=3,'lev_1'=2] {'tile_0'}, dimensions={0}, use_global_device_ids=true | all-gather | bytes 432 | tf_op jit(solution)/shard_map/all_gather | solution.py:27
  35.2 8.4 all-gather.2
  44.2 1.0 convert_reduce_fusion
  45.8 11.7 %cholesky.76 = f32[128,128]{1,0:T(8,128)S(1)} custom-call(f32[128,128]{1,0:T(8,128)S(1)} %cholesky.189), custom_call_target="Cholesky" | custom-call | tf_op jit(solution)/shard_map/jit(cholesky)/cholesky | solution.py:106
  57.5 9.8 custom-call.25
  67.9 11.7 %cholesky.160 = f32[128,128]{1,0:T(8,128)S(1)} custom-call(f32[128,128]{1,0:T(8,128)S(1)} %cholesky.193), custom_call_target="Cholesky" | custom-call | tf_op jit(solution)/shard_map/jit(cholesky)/cholesky | solution.py:106
  79.7 10.0 %custom-call.26 = f32[1,128,128]{1,2,0:T(8,128)S(1)} custom-call(f32[1,128,128]{2,1,0:T(8,128)S(1)} %get-tuple-element.193), custom_call_target="InvertDiagBlocksLowerTriangular" | custom-call | tf_op jit(solution)/shard_map/jit(cholesky)/cholesky | solution.py:106
  90.2 11.7 %cholesky.179 = f32[128,128]{1,0:T(8,128)S(1)} custom-call(f32[128,128]{1,0:T(8,128)S(1)} %convolution_subtract_fusion.1), custom_call_target="Cholesky" | custom-call | tf_op jit(solution)/shard_map/jit(cholesky)/cholesky | solution.py:106
  101.9 0.7 compare_reduce_fusion
  102.6 0.6 compare_reduce_fusion.1
  105.3 6.4 while.16
  105.4 0.6 fusion.147
  106.0 1.4 bitcast_dynamic-update-slice_fusion.2
  107.5 0.6 fusion.147
  108.1 1.4 bitcast_dynamic-update-slice_fusion.2
  109.7 0.6 fusion.147
  110.3 1.4 bitcast_dynamic-update-slice_fusion.2
  111.7 29.5 %custom-call.30 = f32[3,128,128]{1,2,0:T(8,128)S(1)} custom-call(f32[3,128,128]{2,1,0:T(8,128)S(1)} %get-tuple-element.129), custom_call_target="InvertDiagBlocksLowerTriangular" | custom-call | tf_op jit(solution)/shard_map/triangular_solve/custom-call.6 | solution.py:115
  142.4 0.4 convolution_bitcast_fusion.2
  142.7 0.4 fusion.50
  143.7 306.2 %all_gather.18 = f32[2,1,384,129]{3,0,1,2:T(2,128)S(1)} all-gather(f32[2,1,3,129]{3,0,1,2:T(2,128)S(1)} %maximum_bitcast_fusion), channel_id=1, replica_groups=mesh['tile_0'=8,'tile_1'=4,'tile_2'=4,'lev_0'=3,'lev_1'=2] {'tile_0','ti..., dimensions={2}, use_global_device_ids=true | all-gather | bytes 399384 | tf_op jit(solution)/shard_map/all_gather | solution.py:43
  452.1 0.8 constant_dynamic-slice_fusion.2
  453.5 0.4 reshape.603
  454.0 0.6 convolution_bitcast_fusion.5
  454.8 0.8 dynamic-slice_compare_fusion
  456.7 0.6 scatter-add.29
  458.0 11.6 %all-reduce.5 = (f32[2]{0:T(128)S(1)}, f32[2]{0:T(128)S(1)}) all-reduce(f32[2]{0:T(128)S(1)} %get-tuple-element.180, f32[2]{0:T(128)S(1)} %get-tuple-element.176), channel_id=1, replica_groups=mesh['tile_0'=8,'tile_1'=4,'tile_2'=4,'lev_0'=3,'lev_1'=2] {'tile_0'}, use_global_device_ids=true, to_apply=%region_10.13 | all-reduce | flops 4 | bytes 32 | tf_op jit(solution)/shard_map/psum | solution.py:52
  469.5 6.6 all-reduce.9
  476.1 7.3 all-reduce.7
  483.4 14.7 %all-reduce.11 = (f32[2]{0:T(128)S(1)}, f32[2]{0:T(128)S(1)}) all-reduce(f32[2]{0:T(128)S(1)} %get-tuple-element.158, f32[2]{0:T(128)S(1)} %get-tuple-element.159), channel_id=1, replica_groups=mesh['tile_0'=8,'tile_1'=4,'tile_2'=4,'lev_0'=3,'lev_1'=2] {'lev_0'}, use_global_device_ids=true, to_apply=%region_13.16 | all-reduce | flops 4 | bytes 32 | tf_op jit(solution)/shard_map/psum | solution.py:52
  498.1 77.0 %all-reduce.13 = (f32[2]{0:T(128)S(1)}, f32[2]{0:T(128)S(1)}) all-reduce(f32[2]{0:T(128)S(1)} %get-tuple-element.166, f32[2]{0:T(128)S(1)} %get-tuple-element.167), channel_id=1, replica_groups=mesh['tile_0'=8,'tile_1'=4,'tile_2'=4,'lev_0'=3,'lev_1'=2] {'lev_1'}, use_global_device_ids=true, to_apply=%region_14.17 | all-reduce | flops 4 | bytes 32 | tf_op jit(solution)/shard_map/psum | solution.py:52
  575.4 0.4 convolution_bitcast_fusion.1
  575.8 0.4 convolution_divide_fusion
  576.2 0.4 convolution_bitcast_fusion
  576.5 0.4 fusion.45
  577.5 308.2 %all_gather.19 = f32[2,1,384,129]{3,0,1,2:T(2,128)S(1)} all-gather(f32[2,1,3,129]{3,0,1,2:T(2,128)S(1)} %maximum_bitcast_fusion.1), channel_id=1, replica_groups=mesh['tile_0'=8,'tile_1'=4,'tile_2'=4,'lev_0'=3,'lev_1'=2] {'tile_0','ti..., dimensions={2}, use_global_device_ids=true | all-gather | bytes 399384 | tf_op jit(solution)/shard_map/all_gather | solution.py:43
  888.9 0.6 convolution_bitcast_fusion.4
  890.5 0.6 scatter-add.35
  891.7 11.3 %all-reduce.4 = (f32[2]{0:T(128)S(1)}, f32[2]{0:T(128)S(1)}) all-reduce(f32[2]{0:T(128)S(1)} %get-tuple-element.141, f32[2]{0:T(128)S(1)} %get-tuple-element.140), channel_id=1, replica_groups=mesh['tile_0'=8,'tile_1'=4,'tile_2'=4,'lev_0'=3,'lev_1'=2] {'tile_0'}, use_global_device_ids=true, to_apply=%region_23.26 | all-reduce | flops 4 | bytes 32 | tf_op jit(solution)/shard_map/psum | solution.py:52
  902.9 6.6 all-reduce.8
  909.6 6.0 all-reduce.6
  915.6 7.7 all-reduce.10
  923.3 66.3 %all-reduce.12 = (f32[2]{0:T(128)S(1)}, f32[2]{0:T(128)S(1)}) all-reduce(f32[2]{0:T(128)S(1)} %get-tuple-element.164, f32[2]{0:T(128)S(1)} %get-tuple-element.165), channel_id=1, replica_groups=mesh['tile_0'=8,'tile_1'=4,'tile_2'=4,'lev_0'=3,'lev_1'=2] {'lev_1'}, use_global_device_ids=true, to_apply=%region_27.30 | all-reduce | flops 4 | bytes 32 | tf_op jit(solution)/shard_map/psum | solution.py:52
  989.7 0.7 reshape.703
  990.5 0.7 reshape.702
  (143 shorter events, 14.9 us)
Async XLA Ops:
  67.9 73.3 %copy-start = (f32[2,1,3,1024]{3,1,2,0:T(1,128)S(1)}, f32[2,1,3,1024]{3,1,2,0:T(1,128)}, u32[]{:S(2)}) copy-start(f32[2,1,3,1024]{3,1,2,0:T(1,128)} %param.25) | copy-start | bytes 73732
where the time goes:
time: 992 us; the launch traced here: 991 us
  blocking collectives  869 us (88%)
  other arithmetic  91.6 us (9%)
  local copies, waits for them, and re-layouts  16.6 us (2%)
    all_gather x2, blocking collectives, side_by_side(): result = lax.all_gather(both, axis, axis=dim, tiled=True)  614 us
    psum x10, blocking collectives, over_axes(): x = lax.psum(x, axis)  215 us
    another operation x10, other arithmetic, coarse_factor(): return jnp.linalg.cholesky(matrix)  56.4 us
    another operation x6, other arithmetic, coarse_solve(): lax.linalg.triangular_solve(factor, middle, left_side=True, lower=True, t...  29.6 us
    all_gather x2, blocking collectives, gather_in_order(): tiles = lax.all_gather(tiles, axes[k], axis=0, tiled=True)  26.7 us

commit v1 on v0

v1 whole, which is shorter than its diff:
```python
import math

import jax
import jax.numpy as jnp
import numpy as np
from jax import lax
from jax.experimental import pallas as pl
from jax.experimental.pallas import tpu as pltpu
from jax.sharding import PartitionSpec as P

F32 = jnp.float32
BF16 = jnp.bfloat16
SIDE = 32
SUBS = 384
PLANE = 16
COLUMN = 8
LEVS = 6
EACH = 3
FIELDS = 6
ROWS = FIELDS * SIDE

SHIFT = 1.28
SIGMA = 3.0
LOW = 32.0 * 0.06486 + SHIFT
TOP = 32.0 * 8.0 + SHIFT
RHO = 0.7681 / LOW
CHEB = 7


def roll(x, shift, axis):
    return pltpu.roll(x, shift, axis)


def iota(shape, dim):
    return lax.broadcasted_iota(jnp.int32, shape, dim)


def dot(a, b):
    return jnp.dot(a, b, preferred_element_type=F32)


def split(x, n):
    parts = []
    for _ in range(n):
        part = x.astype(BF16)
        parts.append(part)
        x = x - part.astype(F32)
    return parts


def pick(onehot, x):
    a, b, c = split(x, 3)
    return dot(onehot, a) + dot(onehot, b) + dot(onehot, c)


def spread(x, onehot):
    a, b, c = split(x, 3)
    return dot(a, onehot) + dot(b, onehot) + dot(c, onehot)


def mm3(a, b):
    ah, al = a
    bh, bl = b
    return dot(ah, bh) + (dot(ah, bl) + dot(al, bh))


def np_split(x):
    hi = x.astype(np.float32).astype(jnp.bfloat16)
    lo = (x - hi.astype(np.float64)).astype(np.float32).astype(jnp.bfloat16)
    return hi, lo


def polynomial():
    deg = 7
    nodes = np.cos(np.pi * (np.arange(deg + 1) + 0.5) / (deg + 1))
    g = 4.0 * nodes
    x = 128.0 + SHIFT - 32.0 * g

    def cheb(n, t):
        return np.where(
            np.abs(t) <= 1,
            np.cos(n * np.arccos(np.clip(t, -1, 1))),
            np.sign(t) ** n * np.cosh(n * np.arccosh(np.maximum(np.abs(t), 1))),
        )

    def tau(v):
        return (TOP + LOW - 2 * v) / (TOP - LOW)

    top = cheb(deg + 1, tau(0.0))
    vals = (1.0 - cheb(deg + 1, tau(x)) / top) / x
    coef = np.polynomial.polynomial.polyfit(nodes, vals, deg)
    at_one = np.polynomial.polynomial.polyval(1.0, coef)
    const = (1.0 / (SHIFT + SIGMA) - at_one) / SUBS
    return [float(c / 4.0**k) for k, c in enumerate(coef)], float(const), float(1.0 / top)


def constants():
    o = np.arange(SIDE) + 1.0
    step = math.pi / (SIDE + 1.0)
    sine = math.sqrt(2.0 / (SIDE + 1.0)) * np.sin(step * o[:, None] * o[None, :])
    lam = 2.0 - 2.0 * np.cos(step * o)
    s6 = np.kron(np.eye(FIELDS), sine)
    k = np.arange(SIDE)
    bt = np.zeros((SIDE, 4, SIDE))
    bt[k, 0, k] = 1
    bt[k, 2, k] = 1
    bt[31, 1, :] = 1
    bt[0, 3, :] = 1
    bt = bt.reshape(SIDE, 128)
    sr = np.zeros((SIDE, 256))
    sr[:, :SIDE] = sine
    sr[:, 128:] = sine @ bt
    rows = np.arange(ROWS)
    i = rows % SIDE
    field = rows // SIDE
    lanes = np.arange(128)
    side, kk = lanes // SIDE, lanes % SIDE
    mask2 = (
        ((side == 0)[None] & (i == 0)[:, None])
        | ((side == 2)[None] & (i == 31)[:, None])
        | (((side == 1) | (side == 3))[None] & (kk[None] == i[:, None]))
    )
    grp = field[None, :] == np.arange(8)[:, None]
    m = np.arange(SUBS)
    cmp = ((lanes // 8)[:, None] == (m // EACH % PLANE)[None]) & ((lanes % 8)[:, None] == (m % EACH)[None])
    rev = (side[:, None] == side[None]) & (kk[:, None] == 31 - kk[None])
    oo = np.arange(32)
    op, os_ = oo // 16, oo % 16
    n = field % EACH
    gp = ((field // EACH)[:, None] == op[None]) & (
        ((os_ < 12)[None] & ((os_ // 4)[None] == n[:, None])) | ((os_ - 12)[None] == n[:, None])
    )
    o16 = np.arange(16)
    lm = np.zeros((16, 256))
    lm[:, :128] = (o16 < 12)[:, None] & ((o16 % 4)[:, None] == side[None])
    lm[:, 128:] = ((o16 >= 12) & (o16 < 15))[:, None]
    b16 = lambda a: a.astype(np.float32).astype(jnp.bfloat16)
    f32 = lambda a: a.astype(np.float32)
    inv = 1.0 / (lam[:, None] + lam[None, :])
    return dict(
        s6=np_split(s6),
        s=np_split(sine),
        sr=np_split(sr),
        inv=(f32(np.tile(inv, (FIELDS, 1))),),
        mask2=(f32(mask2),),
        grp=(b16(grp),),
        grpt=(b16(grp.T),),
        bm=(b16(bt.T),),
        cmp=(b16(cmp),),
        rev=(b16(rev),),
        gp=(b16(gp),),
        lm=(f32(lm),),
    )


def local_part(r, c):
    v = mm3(c["s6"], split(r, 2))
    v = mm3(split(v, 2), c["s"]) * c["inv"][0]
    v = mm3(split(v, 2), c["sr"])
    v = mm3(c["s6"], split(v, 2))
    rims = pick(c["grp"][0], v[:, 128:] * c["mask2"][0])
    return v[:, :SIDE], rims


def packed(v, q, per):
    total = jnp.sum(v, axis=1, keepdims=True)
    shape = (v.shape[0], 128)
    at = iota(shape, 1) == q * 8 + lax.shift_right_logical(iota(shape, 0), 5)
    return jnp.sum(jnp.where(at, total, 0.0), axis=0, keepdims=True)


def tile_a(rims, sums, mass):
    row = iota((8, 128), 0)
    return jnp.where(row == 6, sums, jnp.where(row == 7, mass, rims))


def choose_matrix(colidx):
    return (iota((256, 512), 1) == colidx).astype(BF16)


def tiles_b(buf, choose):
    flat = buf.reshape(128, 128)
    turned = jnp.concatenate([flat] + [roll(flat, 32 * t, 1) for t in (1, 2, 3)], axis=0)
    got = pick(choose, turned)
    group = lax.shift_right_logical(iota((64, 128), 1), 5)
    out = jnp.where(group == 0, got[:64], 0.0)
    for s in (1, 2, 3):
        out = jnp.where(group == s, got[64 * s : 64 * s + 64], out)
    row = iota((8, 128), 0)
    plane = jnp.where(row >= 6, jnp.sum(buf, axis=0), 0.0)
    return out.reshape(8, 8, 128) + plane[None]


def graph(nb):
    lane = iota((SUBS, SUBS), 1)
    total = jnp.zeros((SUBS, SUBS), F32)
    for s in range(4):
        total = total + (nb[:, s : s + 1] == lane).astype(F32)
    return total


def start_inverse(g32):
    coef, const, rho = polynomial()
    g = g32.astype(BF16)
    g2 = dot(g, g)
    g2b = g2.astype(BF16)
    g3 = dot(g2b, g)
    g4 = dot(g2b, g2b)
    g3b, g4b = g3.astype(BF16), g4.astype(BF16)
    eye = (iota((SUBS, SUBS), 0) == iota((SUBS, SUBS), 1)).astype(F32)
    x = coef[0] * eye + const + coef[1] * g32 + coef[2] * g2 + coef[3] * g3 + coef[4] * g4
    x = x + coef[5] * dot(g4b, g) + coef[6] * dot(g4b, g2b) + coef[7] * dot(g4b, g3b)
    return x, rho


def newton(x, g, rho, last):
    xs = split(x, 3)
    gx = dot(g, xs[0]) + (dot(g, xs[1]) + dot(g, xs[2]))
    ones = (SIGMA / SUBS) * jnp.sum(x, axis=0, keepdims=True)
    eye = (iota((SUBS, SUBS), 0) == iota((SUBS, SUBS), 1)).astype(F32)
    rest = eye - ((128.0 + SHIFT) * x - 32.0 * gx + ones)
    x = x + mm3(xs[:2], split(rest, 2))
    if last:
        return x, 0.0
    scale = 2.0 / (2.0 - rho * rho)
    return scale * x, rho * rho / (2.0 - rho * rho)


def wanted_rows(eidx):
    lane = iota((16, SUBS), 1)
    plus = (eidx[:, 0:1] == lane).astype(F32)
    minus = (eidx[:, 1:2] == lane).astype(F32)
    ones = (iota((16, SUBS), 0) == 15).astype(F32)
    return (plus - minus + ones).astype(BF16)


def to_vectors(slots, c):
    wide = spread(slots, c["cmp"][0])
    rows = []
    for k in range(slots.shape[0] // 8):
        row, lane = iota((8, SUBS), 0), iota((8, SUBS), 1)
        keep = (lane >= row * 48) & (lane < row * 48 + 48)
        rows.append(jnp.sum(jnp.where(keep, wide[8 * k : 8 * k + 8], 0.0), axis=0, keepdims=True))
    return rows


def inverse_rows(first, xh, xl, mass):
    delta = mass - SHIFT

    def apply(d, fine):
        e = d * delta
        eh, el = split(e, 2)
        if fine:
            return d + (dot(eh, xh) + (dot(el, xh) + dot(eh, xl)))
        return d + dot(eh, xh)

    sig = 1.0 / RHO
    rk = 1.0 / sig
    rest = first
    d = rest
    y = d
    for k in range(CHEB):
        rest = rest - apply(d, k < 4)
        nxt = 1.0 / (2.0 * sig - rk)
        d = (nxt * rk) * d + (2.0 * nxt / RHO) * rest
        y = y + d
        rk = nxt
    u = y[15:16]
    t = jnp.sum(u, axis=1, keepdims=True)
    w = jnp.sum(y, axis=1, keepdims=True)
    share = (SIGMA / SUBS) / (1.0 - (SIGMA / SUBS) * t)
    return y + (w * share) * u


def coarse_edges(y, s0, s1, c):
    parts = []
    for s in (s0, s1):
        parts.append(jnp.sum(y * s, axis=1, keepdims=True) * c["lm"][0])
    return jnp.concatenate(parts, axis=0)


def finish(r, local, mass2, rims, flip, y, s0, s1, c):
    turned = spread(rims, c["rev"][0])
    rims = jnp.where(flip > 0.5, turned, rims)
    w = coarse_edges(y, s0, s1, c)
    wide = pick(c["gp"][0], w)
    edges = wide[:, :128] - pick(c["grpt"][0], rims)
    z = local + wide[:, 128 : 128 + SIDE]
    image = r + mass2 * z + spread(edges * c["mask2"][0], c["bm"][0])
    return z, image


def dots_row(pairs):
    rows = []
    for p in range(2):
        for a, b in pairs:
            half = slice(96 * p, 96 * p + 96)
            rows.append(jnp.sum(a[half] * b[half], axis=0, keepdims=True))
    block = jnp.concatenate(rows + [jnp.zeros((16 - len(rows), SIDE), F32)], axis=0)
    col = jnp.sum(block, axis=1, keepdims=True)
    at = iota((16, 128), 0) == iota((16, 128), 1)
    return jnp.sum(jnp.where(at, col, 0.0), axis=0, keepdims=True)


def steps(row, p):
    ga, de, rw, qw, zv, wv = [row[:, 6 * p + k : 6 * p + k + 1] for k in range(6)]
    a0 = ga / de
    g1 = ga - a0 * (de + rw) + a0 * a0 * qw
    d1 = de - a0 * (qw + zv) + a0 * a0 * wv
    beta = g1 / ga
    cross = de - a0 * (0.5 * (qw + zv))
    den = d1 + 2.0 * beta * cross + beta * beta * de
    a1 = g1 / den
    return a0 + a1 * (1.0 + beta), a1 * a0


def kernel(names, *refs):
    ins = refs[: 6 + sum(k for _, k in names)]
    r_ref, mass_ref, nb_ref, col_ref, eidx_ref, flip_ref = ins[:6]
    c, at = {}, 6
    for name, k in names:
        c[name] = [ref[...] for ref in ins[at : at + k]]
        at += k
    sol_ref, res_ref = refs[at : at + 2]
    (stga0, stga1, bufa0, bufa1, stgb0, stgb1, bufb0, bufb1) = refs[at + 2 : at + 10]
    (st3a, st3b, st3c, buf3a, buf3b, buf3c) = refs[at + 10 : at + 16]
    ssem, rsem = refs[at + 16 :]

    t = lax.axis_index("tile")
    lev = lax.axis_index("lev")
    plane = t // PLANE
    q = t % PLANE

    def peer_a(k):
        return (plane * PLANE + (q + k) % PLANE, lev)

    def peer_b(k):
        return (((plane + k) % COLUMN) * PLANE + q, lev)

    def peer_c(k):
        return (t, (lev + k) % LEVS)

    groups = ((peer_a, PLANE), (peer_b, COLUMN), (peer_c, LEVS))

    barrier = pltpu.get_barrier_semaphore()
    for peer, size in groups:
        for k in range(1, size):
            pl.semaphore_signal(barrier, 1, device_id=peer(k), device_id_type=pl.DeviceIdType.MESH)

    def send(group, src_of, dst, n):
        peer, size = groups[group]
        for k in range(1, size):
            target = peer(k)
            pltpu.make_async_remote_copy(
                src_ref=src_of(k), dst_ref=dst, send_sem=ssem.at[n], recv_sem=rsem.at[n],
                device_id=target, device_id_type=pl.DeviceIdType.MESH,
            ).start()

    def done(group, buf, n, recv):
        peer, size = groups[group]
        view = buf.at[pl.ds(0, size - 1)]
        copy = pltpu.make_async_remote_copy(
            src_ref=view, dst_ref=view, send_sem=ssem.at[n], recv_sem=rsem.at[n],
            device_id=peer(1), device_id_type=pl.DeviceIdType.MESH,
        )
        if recv:
            copy.wait_recv()
        else:
            copy.wait_send()

    r = r_ref[...]
    mass = mass_ref[...]
    mass2 = jnp.concatenate([mass, mass], axis=0)
    zrow = jnp.zeros((1, 128), F32)

    l0, rims = local_part(r, c)
    tile = tile_a(rims, packed(r, q, 0), packed(mass, q, 0))
    stga0[...] = tile
    bufa0[q] = tile
    pl.semaphore_wait(barrier, (PLANE - 1) + (COLUMN - 1) + (LEVS - 1))
    send(0, lambda k: stga0, bufa0.at[q], 0)

    choose = choose_matrix(col_ref[...])
    g32 = graph(nb_ref[...])
    x, rho = start_inverse(g32)
    g = g32.astype(BF16)

    done(0, bufa0, 0, True)
    stgb0[...] = tiles_b(bufa0[...], choose)
    bufb0[plane] = stgb0[plane]
    send(1, lambda k: stgb0.at[(plane + k) % COLUMN], bufb0.at[plane], 1)

    x, rho = newton(x, g, rho, False)
    x, rho = newton(x, g, rho, False)
    x, rho = newton(x, g, rho, True)
    xs = split(x, 3)
    e0 = wanted_rows(eidx_ref[...])
    first = dot(e0, xs[0]) + (dot(e0, xs[1]) + dot(e0, xs[2]))
    flip = flip_ref[...]

    done(1, bufb0, 1, True)
    got = bufb0[...]
    sums = bufb0[:, 6, :]
    masses = bufb0[:, 7, :]
    three = jnp.concatenate([masses, sums, roll(sums, 128 - EACH, 1)], axis=0)
    dvec, s0, s1 = to_vectors(three, c)
    y = inverse_rows(first, xs[0], xs[1], dvec)
    z0, q0 = finish(r, l0, mass2, jnp.sum(got, axis=0), flip, y, s0, s1, c)

    l1, rims = local_part(q0, c)
    tile = tile_a(rims, packed(q0, q, 0), zrow)
    stga1[...] = tile
    bufa1[q] = tile
    send(0, lambda k: stga1, bufa1.at[q], 2)
    done(0, bufa1, 2, True)
    stgb1[...] = tiles_b(bufa1[...], choose)
    bufb1[plane] = stgb1[plane]
    send(1, lambda k: stgb1.at[(plane + k) % COLUMN], bufb1.at[plane], 3)
    done(1, bufb1, 3, True)
    got = bufb1[...]
    sums = bufb1[:, 6, :]
    two = jnp.concatenate([sums, roll(sums, 128 - EACH, 1)], axis=0)
    s0, s1 = to_vectors(two, c)
    w, v = finish(q0, l1, mass2, jnp.sum(got, axis=0), flip, y, s0, s1, c)

    row = dots_row(((r, z0), (z0, q0), (r, w), (q0, w), (z0, v), (w, v)))
    for n, (group, me, stg, buf) in enumerate(
        ((0, q, st3a, buf3a), (1, plane, st3b, buf3b), (2, lev, st3c, buf3c))
    ):
        stg[...] = row
        buf[me] = row
        send(group, lambda k: stg, buf.at[me], 4 + n)
        done(group, buf, 4 + n, True)
        row = jnp.sum(buf[...], axis=0)

    for p in range(2):
        a, b = steps(row, p)
        half = slice(96 * p, 96 * p + 96)
        sol_ref[half, :] = a * z0[half] - b * w[half]
        res_ref[half, :] = r[half] - a * q0[half] + b * v[half]

    done(0, bufa0, 0, False)
    done(1, bufb0, 1, False)
    done(0, bufa1, 2, False)
    done(1, bufb1, 3, False)
    done(0, buf3a, 4, False)
    done(1, buf3b, 5, False)
    done(2, buf3c, 6, False)


def tables(neighbour_sub, neighbour_side, side_flip, t):
    plane, q = t // PLANE, t % PLANE

    def mine(a):
        return lax.dynamic_index_in_dim(a.reshape(COLUMN, PLANE, EACH, 4), q, 1, keepdims=False)

    nb, ns = mine(neighbour_sub), mine(neighbour_side)
    device = nb // EACH
    inside = device // PLANE == plane
    src = (device % PLANE) * 8 + nb % EACH
    turn = (jnp.arange(4, dtype=jnp.int32) - ns) % 4
    col = jnp.where(inside, turn * 128 + src, -1024)
    col = jnp.stack([col, col + EACH], axis=1).reshape(COLUMN, FIELDS, 4)
    col = jnp.pad(col, ((0, 0), (0, 2), (0, 0)), constant_values=-1)
    col = jnp.moveaxis(col, 2, 0).reshape(256, 1)
    own = t * EACH + jnp.arange(EACH, dtype=jnp.int32)
    mynb = lax.dynamic_slice_in_dim(neighbour_sub, t * EACH, EACH, 0)
    plus = jnp.concatenate([jnp.repeat(own, 4), own, jnp.full((1,), -1, jnp.int32)])
    minus = jnp.concatenate([mynb.reshape(-1), jnp.full((4,), -1, jnp.int32)])
    myflip = lax.dynamic_slice_in_dim(side_flip, t * EACH, EACH, 0).astype(F32)
    flip = jnp.repeat(myflip, SIDE, axis=1)
    flip = jnp.concatenate([flip, flip, jnp.zeros((2, 128), F32)], axis=0)
    return col, jnp.stack([plus, minus], axis=1), flip


def shards(sources, mass_coef, neighbour_sub, neighbour_side, side_flip):
    t = lax.axis_index("tile")
    col, eidx, flip = tables(neighbour_sub, neighbour_side, side_flip, t)
    consts = constants()
    names = tuple((k, len(v)) for k, v in consts.items())
    flat = [jnp.asarray(a) for v in consts.values() for a in v]
    vm = pl.BlockSpec(memory_space=pltpu.VMEM)
    args = [sources.reshape(ROWS, SIDE), mass_coef.reshape(EACH * SIDE, SIDE), neighbour_sub, col, eidx, flip, *flat]
    scratch = [
        pltpu.VMEM((8, 128), F32), pltpu.VMEM((8, 128), F32),
        pltpu.VMEM((PLANE, 8, 128), F32), pltpu.VMEM((PLANE, 8, 128), F32),
        pltpu.VMEM((COLUMN, 8, 128), F32), pltpu.VMEM((COLUMN, 8, 128), F32),
        pltpu.VMEM((COLUMN, 8, 128), F32), pltpu.VMEM((COLUMN, 8, 128), F32),
        pltpu.VMEM((1, 128), F32), pltpu.VMEM((1, 128), F32), pltpu.VMEM((1, 128), F32),
        pltpu.VMEM((PLANE, 1, 128), F32), pltpu.VMEM((COLUMN, 1, 128), F32), pltpu.VMEM((LEVS, 1, 128), F32),
        pltpu.SemaphoreType.DMA((7,)), pltpu.SemaphoreType.DMA((7,)),
    ]
    out = jax.ShapeDtypeStruct((ROWS, SIDE), F32)
    sol, res = pl.pallas_call(
        lambda *refs: kernel(names, *refs),
        out_shape=(out, out),
        in_specs=[vm] * len(args),
        out_specs=(vm, vm),
        scratch_shapes=scratch,
        compiler_params=pltpu.CompilerParams(collective_id=0, has_side_effects=True, vmem_limit_bytes=48 << 20),
        name="schwarz",
    )(*args)
    return sol.reshape(sources.shape), res.reshape(sources.shape)


def solution(mesh):
    placed = (P(None, "lev", "tile", None), P("tile", None), P(), P(), P())
    return jax.shard_map(
        shards,
        mesh=mesh,
        in_specs=placed,
        out_specs=(P(None, "lev", "tile", None), P(None, "lev", "tile", None)),
        check_vma=False,
    )
```

time: 992 us -> 70.7 us (0.07)
  blocking collectives: 869 us -> 0 us
  other arithmetic: 91.6 us -> 1.05 us
  Pallas kernels: 0 us -> 63.3 us
  local copies, waits for them, and re-layouts: 16.6 us -> 5.2 us
    all_gather x4 -> x0, blocking collectives: 641 us -> none  [the longest x2 614 us: side_by_side(): result = lax.all_gather(both, axis, axis=dim, tiled=True)]
    psum x10 -> x0, blocking collectives: 215 us -> none  [over_axes(): x = lax.psum(x, axis)]
    another operation x18 -> x3, other arithmetic: 86 us -> 0.1 us  [the longest x2 0.09 us: tables(): return (col, jnp.stack([plus, minus], axis=1), flip)]
    pallas_call x0 -> x1, Pallas kernels: none -> 63.3 us  [shards(): pl.pallas_call(lambda *refs: kernel(names, *refs), out_shape=(out, out),...]
    unnamed x1 -> x0, blocking collectives: 13.1 us -> none
where the time goes in v1:
time: 70.7 us; the launch traced here: 70.4 us
  Pallas kernels  63.3 us (90%)
  local copies, waits for them, and re-layouts  5.2 us (7%)
  other arithmetic  1.05 us (1%)
  between operations  0.92 us (1%)
    pallas_call x1, Pallas kernels, shards(): pl.pallas_call(lambda *refs: kernel(names, *refs), out_shape=(out, out),...  63.3 us
    unnamed x41, local copies, waits for them, and re-layouts  2.21 us
    reshape x2, local copies, waits for them, and re-layouts, shards(): return (sol.reshape(sources.shape), res.reshape(sources.shape))  1.43 us

profile of v1, /device:TPU:1, one launch (start us, length us, event | category | flops | bytes accessed | tf_op | source)
XLA Modules:
  0.0 70.4 jit_solution(16781605770588486926)
XLA Ops:
  0.6 0.0 copy-start.15
  0.7 0.7 copy-done.15
  1.3 0.2 reshape.39
  1.6 0.5 copy-done.18
  2.0 0.2 reshape.40
  2.3 0.1 copy.59
  2.4 0.1 copy.60
  2.5 0.0 copy-start.16
  2.6 0.0 copy-start.17
  2.6 0.0 copy-start.13
  2.6 0.0 copy-start.10
  2.6 0.0 copy-start.11
  2.6 0.1 copy.51
  2.7 0.0 copy-start.12
  2.7 0.1 reshape.48.refs_3_
  2.8 0.0 copy-start.7
  2.8 0.8 %dynamic-slice_convert_fusion = (f32[3,4]{0,1:T(4,128)S(1)}, s32[3,4]{0,1:T(4,128)S(1)}) fusion(s32[384,4]{0,1:T(4,128)} %param.24, s32[]{:T(128)S(6)} %select_n.67, s32[384,4]{0,1:T(4,128)S(1)} %copy-done.15), kind=kLoop, calls=%fused_computation.26 | loop fusion | flops 12 | bytes 196 | tf_op jit(solution)/shard_map/convert_element_type | solution.py:470
  3.6 0.1 copy.52
  3.7 0.1 reshape.44
  3.8 0.1 broadcast_in_dim.15
  3.9 0.1 reshape.43
  3.9 0.1 add_bitcast_fusion
  4.0 0.0 copy-start.4
  4.1 0.1 copy.56.refs_4_
  4.1 0.1 copy.53
  4.2 0.1 broadcast_in_dim.16
  4.3 0.1 reshape.45
  4.4 0.1 pad.8.clone
  4.5 0.1 maximum_maximum_fusion.refs_5_
  4.5 0.1 copy.54.refs_2_
  4.7 0.0 copy-done.16
  4.7 0.0 copy-start.1
  4.7 0.1 reduce
  4.8 0.0 copy-start
  4.8 0.1 reshape.37.refs_0_
  4.9 0.0 copy-done.17
  4.9 0.0 copy-start.14
  4.9 0.1 reshape.38.refs_1_
  5.0 0.0 copy-done.13
  5.0 0.0 copy-done.10
  5.1 0.4 copy-done.2
  5.5 0.0 copy-done.3
  5.5 0.1 copy-done.1
  5.6 0.1 copy-done
  5.7 0.0 copy-done.14
  5.7 63.3 %schwarz.1 = (f32[192,32]{1,0:T(8,128)S(1)}, f32[192,32]{1,0:T(8,128)S(1)}) custom-call(f32[192,32]{1,0:T(8,128)S(1)} %reshape.37.refs_0_, f32[96,32]{1,0:T(8,128)S(1)} %reshape.38.refs_1_, s32[384,4]{1,0:T(8,128)S(1)} %copy.54.refs_2_, s32[256,1]{1,0:T(8,128)S(1)} %reshape.48.refs_3_, s32[16,2]{1,0:T(8,128)S(1)} %copy.56.refs_4_, ...), custom_call_target="tpu_custom_call" | custom-call | tf_op jit(solution)/shard_map/schwarz/pallas_call | solution.py:494
  69.0 0.7 %reshape.49 = f32[2,1,3,1024]{3,1,2,0:T(1,128)} reshape(f32[192,32]{1,0:T(8,128)S(1)} %get-tuple-element.4) | data formatting | bytes 49152 | tf_op jit(solution)/shard_map/reshape | solution.py:503
  69.7 0.7 %reshape.50 = f32[2,1,3,1024]{3,1,2,0:T(1,128)} reshape(f32[192,32]{1,0:T(8,128)S(1)} %get-tuple-element.5) | data formatting | bytes 49152 | tf_op jit(solution)/shard_map/reshape | solution.py:503
  (23 shorter events, 0.1 us)
Async XLA Ops:
  0.6 0.7 copy-start.15
  1.3 0.7 copy-start.18
  2.5 2.2 %copy-start.16 = (f32[2,1,3,1024]{3,1,2,0:T(1,128)S(1)}, f32[2,1,3,1024]{3,1,2,0:T(1,128)}, u32[]{:S(2)}) copy-start(f32[2,1,3,1024]{3,1,2,0:T(1,128)} %param.20) | copy-start | bytes 73732
  2.6 2.3 %copy-start.17 = (f32[3,1024]{1,0:T(4,128)S(1)}, f32[3,1024]{1,0:T(4,128)}, u32[]{:S(2)}) copy-start(f32[3,1024]{1,0:T(4,128)} %param.21) | copy-start | bytes 36868
  2.6 2.4 %copy-start.13 = (bf16[32,32]{1,0:T(8,128)(2,1)S(1)}, bf16[32,32]{1,0:T(8,128)(2,1)}, u32[]{:S(2)}) copy-start(bf16[32,32]{1,0:T(8,128)(2,1)} %constant.124.clone.refs_9_) | copy-start | bytes 6148
  2.6 2.4 %copy-start.10 = (bf16[32,256]{1,0:T(8,128)(2,1)S(1)}, bf16[32,256]{1,0:T(8,128)(2,1)}, u32[]{:S(2)}) copy-start(bf16[32,256]{1,0:T(8,128)(2,1)} %constant.126.clone.refs_11_) | copy-start | bytes 49156
  2.6 2.4 %copy-start.11 = (f32[16,256]{1,0:T(8,128)S(1)}, f32[16,256]{1,0:T(8,128)}, u32[]{:S(2)}) copy-start(f32[16,256]{1,0:T(8,128)} %constant.135.clone.refs_20_) | copy-start | bytes 49156
  2.7 2.3 %copy-start.5 = (bf16[192,8]{1,0:T(8,128)(2,1)S(1)}, bf16[192,8]{1,0:T(8,128)(2,1)}, u32[]{:S(2)}) copy-start(bf16[192,8]{1,0:T(8,128)(2,1)} %constant.130.clone.refs_15_) | copy-start | bytes 9220
  2.7 2.3 %copy-start.6 = (bf16[192,32]{1,0:T(8,128)(2,1)S(1)}, bf16[192,32]{1,0:T(8,128)(2,1)}, u32[]{:S(2)}) copy-start(bf16[192,32]{1,0:T(8,128)(2,1)} %constant.134.clone.refs_19_) | copy-start | bytes 36868
  2.7 2.3 %copy-start.8 = (bf16[128,128]{1,0:T(8,128)(2,1)S(1)}, bf16[128,128]{1,0:T(8,128)(2,1)}, u32[]{:S(2)}) copy-start(bf16[128,128]{1,0:T(8,128)(2,1)} %constant.133.clone.refs_18_) | copy-start | bytes 98308
  2.7 2.4 %copy-start.9 = (bf16[32,256]{1,0:T(8,128)(2,1)S(1)}, bf16[32,256]{1,0:T(8,128)(2,1)}, u32[]{:S(2)}) copy-start(bf16[32,256]{1,0:T(8,128)(2,1)} %constant.125.clone.refs_10_) | copy-start | bytes 49156
  2.7 2.4 %copy-start.12 = (bf16[32,32]{1,0:T(8,128)(2,1)S(1)}, bf16[32,32]{1,0:T(8,128)(2,1)}, u32[]{:S(2)}) copy-start(bf16[32,32]{1,0:T(8,128)(2,1)} %constant.123.clone.refs_8_) | copy-start | bytes 6148
  2.8 2.3 %copy-start.7 = (bf16[128,32]{1,0:T(8,128)(2,1)S(1)}, bf16[128,32]{1,0:T(8,128)(2,1)}, u32[]{:S(2)}) copy-start(bf16[128,32]{1,0:T(8,128)(2,1)} %constant.131.clone.refs_16_) | copy-start | bytes 24580
  4.0 1.0 %copy-start.4 = (bf16[128,384]{1,0:T(8,128)(2,1)S(1)}, bf16[128,384]{1,0:T(8,128)(2,1)}, u32[]{:S(2)}) copy-start(bf16[128,384]{1,0:T(8,128)(2,1)} %constant.132.clone.refs_17_) | copy-start | bytes 294916
  4.5 0.9 %copy-start.2 = (f32[192,32]{1,0:T(8,128)S(1)}, f32[192,32]{1,0:T(8,128)}, u32[]{:S(2)}) copy-start(f32[192,32]{1,0:T(8,128)} %constant.127.clone.refs_12_) | copy-start | bytes 73732
  4.5 1.0 %copy-start.3 = (f32[192,128]{1,0:T(8,128)S(1)}, f32[192,128]{1,0:T(8,128)}, u32[]{:S(2)}) copy-start(f32[192,128]{1,0:T(8,128)} %constant.128.clone.refs_13_) | copy-start | bytes 294916
  4.7 0.9 %copy-start.1 = (bf16[192,192]{1,0:T(8,128)(2,1)S(1)}, bf16[192,192]{1,0:T(8,128)(2,1)}, u32[]{:S(2)}) copy-start(bf16[192,192]{1,0:T(8,128)(2,1)} %constant.122.clone.refs_7_) | copy-start | bytes 221188
  4.8 0.9 %copy-start = (bf16[192,192]{1,0:T(8,128)(2,1)S(1)}, bf16[192,192]{1,0:T(8,128)(2,1)}, u32[]{:S(2)}) copy-start(bf16[192,192]{1,0:T(8,128)(2,1)} %constant.121.clone.refs_6_) | copy-start | bytes 221188
  4.9 0.8 %copy-start.14 = (bf16[8,192]{1,0:T(8,128)(2,1)S(1)}, bf16[8,192]{1,0:T(8,128)(2,1)}, u32[]{:S(2)}) copy-start(bf16[8,192]{1,0:T(8,128)(2,1)} %constant.129.clone.refs_14_) | copy-start | bytes 9220

commit v2 on v1

v2 whole, which is shorter than its diff:
```python
import math

import jax
import jax.numpy as jnp
import numpy as np
from jax import lax
from jax.experimental import pallas as pl
from jax.experimental.pallas import tpu as pltpu
from jax.sharding import PartitionSpec as P

F32 = jnp.float32
BF16 = jnp.bfloat16
SIDE = 32
SUBS = 384
PLANE = 16
COLUMN = 8
LEVS = 6
EACH = 3
LINE = 4
ROWS = 8 * SIDE

SHIFT = 1.28
SIGMA = 3.0
LOW = 32.0 * 0.06486 + SHIFT
TOP = 32.0 * 8.0 + SHIFT
RHO = 0.7681 / LOW
CHEB = 7


def roll(x, shift, axis):
    return pltpu.roll(x, shift, axis)


def iota(shape, dim):
    return lax.broadcasted_iota(jnp.int32, shape, dim)


def dot(a, b):
    return jnp.dot(a, b, preferred_element_type=F32)


def split(x, n):
    parts = []
    for _ in range(n):
        part = x.astype(BF16)
        parts.append(part)
        x = x - part.astype(F32)
    return parts


def pick(onehot, x):
    a, b, c = split(x, 3)
    return dot(onehot, a) + dot(onehot, b) + dot(onehot, c)


def spread(x, onehot):
    a, b, c = split(x, 3)
    return dot(a, onehot) + dot(b, onehot) + dot(c, onehot)


def mm3(a, b):
    ah, al = a
    bh, bl = b
    return dot(ah, bh) + (dot(ah, bl) + dot(al, bh))


def np_split(x):
    hi = x.astype(np.float32).astype(jnp.bfloat16)
    lo = (x - hi.astype(np.float64)).astype(np.float32).astype(jnp.bfloat16)
    return hi, lo


def polynomial():
    deg = 7
    nodes = np.cos(np.pi * (np.arange(deg + 1) + 0.5) / (deg + 1))
    g = 4.0 * nodes
    x = 128.0 + SHIFT - 32.0 * g

    def cheb(n, t):
        return np.where(
            np.abs(t) <= 1,
            np.cos(n * np.arccos(np.clip(t, -1, 1))),
            np.sign(t) ** n * np.cosh(n * np.arccosh(np.maximum(np.abs(t), 1))),
        )

    def tau(v):
        return (TOP + LOW - 2 * v) / (TOP - LOW)

    top = cheb(deg + 1, tau(0.0))
    vals = (1.0 - cheb(deg + 1, tau(x)) / top) / x
    coef = np.polynomial.polynomial.polyfit(nodes, vals, deg)
    at_one = np.polynomial.polynomial.polyval(1.0, coef)
    const = (1.0 / (SHIFT + SIGMA) - at_one) / SUBS
    return [float(c / 4.0**k) for k, c in enumerate(coef)], float(const), float(1.0 / top)


def constants():
    o = np.arange(SIDE) + 1.0
    step = math.pi / (SIDE + 1.0)
    sine = math.sqrt(2.0 / (SIDE + 1.0)) * np.sin(step * o[:, None] * o[None, :])
    lam = 2.0 - 2.0 * np.cos(step * o)
    inv = np.repeat(1.0 / (lam[:, None] + lam[None, :]), 8, axis=0)
    lanes = np.arange(128)
    side, kk = lanes // SIDE, lanes % SIDE
    m = np.arange(SUBS)
    cmp = ((lanes // 8)[:, None] == (m // EACH % PLANE)[None]) & ((lanes % 8)[:, None] == (m % EACH)[None])
    rev = (side[:, None] == side[None]) & (kk[:, None] == 31 - kk[None])
    s8 = np.concatenate(np_split(np.kron(sine, np.eye(8))), axis=0)
    s = np.concatenate([np.pad(a, ((0, 0), (0, 128 - SIDE))) for a in np_split(sine)], axis=0)
    small = np.concatenate([s, rev.astype(np.float32).astype(jnp.bfloat16)], axis=0)
    wide = cmp.astype(np.float32).astype(jnp.bfloat16)
    return s8, small, wide, inv.astype(np.float32)


def by_row(v):
    return v.reshape(SIDE, 8, 128)


def stack_fields(first, second):
    return jnp.concatenate([first, second, jnp.zeros((2, first.shape[1]), F32)], axis=0)


def to_field(x):
    lane = iota((8, 128), 1)
    rows = []
    for i in range(SIDE):
        g, h = i // 4, i % 4
        part = x[:, 128 * g : 128 * g + 128]
        part = part if h == 0 else roll(part, 128 - 32 * h, 1)
        rows.append(jnp.where(lane < SIDE, part, 0.0))
    return jnp.concatenate(rows, axis=0)


def from_field(v):
    parts = []
    for g in range(8):
        total = v[4 * g]
        for h in (1, 2, 3):
            total = total + roll(v[4 * g + h], 32 * h, 1)
        parts.append(total)
    return jnp.concatenate(parts, axis=1)


def local_part(r, c):
    v = mm3(c["s8"], split(r[:, :SIDE], 2))
    v = mm3(split(v, 2), c["s"])[:, :SIDE] * c["inv"]
    v = mm3(split(v, 2), c["s"])
    v = mm3(c["s8"], split(v, 2))
    f = by_row(v)
    lane = iota((8, 128), 1)
    right = jnp.zeros((8, 128), F32)
    left = jnp.zeros((8, 128), F32)
    for i in range(SIDE):
        moved = roll(f[i], i + 1, 1)
        right = jnp.where(lane == 32 + i, moved, right)
        left = jnp.where(lane == 1 + i, moved, left)
    rims = (f[0] + roll(f[31], 64, 1)) + (right + roll(left, 95, 1))
    return v, rims


def packed(v, q):
    total = jnp.sum(jnp.sum(by_row(v), axis=0), axis=1, keepdims=True)
    at = iota((8, 128), 1) == q * 8 + iota((8, 128), 0)
    return jnp.sum(jnp.where(at, total, 0.0), axis=0, keepdims=True)


def tile_a(rims, sums, mass):
    row = iota((8, 128), 0)
    return jnp.where(row == 6, sums, jnp.where(row == 7, mass, rims))


def tables(nb, ns, fl, t):
    plane, q = t // PLANE, t % PLANE
    row, lane = iota((72, SUBS), 0), iota((72, SUBS), 1)
    y = jnp.where(row < 64, lax.shift_right_logical(row, jnp.int32(3)), plane)
    field = row & 7
    sub = (y * PLANE + q) * EACH + jnp.where(field >= EACH, field - EACH, field)
    take = (lane == sub) & (field < 6)

    def column(a, s):
        return jnp.sum(jnp.where(take, a[s : s + 1].astype(F32), 0.0), axis=1, keepdims=True)

    nbs = [column(nb, s).astype(jnp.int32) for s in range(4)]
    nss = [column(ns, s).astype(jnp.int32) for s in range(4)]
    fls = [column(fl, s) for s in range(4)]

    field = iota((64, 1), 0) & 7
    third = jnp.where(field >= EACH, EACH, 0)
    cols = iota((64, 512), 1)
    choose = []
    for s in range(4):
        sub = nbs[s][:64]
        device = lax.shift_right_logical(sub * 21846, jnp.int32(16))
        at = ((s - nss[s][:64]) & 3) * 128 + (device & 15) * 8 + (sub - EACH * device) + third
        inside = (lax.shift_right_logical(device, jnp.int32(4)) == plane) & (field < 6)
        choose.append((cols == jnp.where(inside, at, -1)).astype(F32).astype(BF16))

    field, lane = iota((8, SUBS), 0), iota((8, SUBS), 1)
    own = (lane == t * EACH + jnp.where(field >= EACH, field - EACH, field)).astype(F32)
    rows = []
    for s in range(4):
        rows.append(jnp.where(field < 6, own - (lane == nbs[s][64:72]).astype(F32), 0.0))
    rows.append(jnp.where(field < 6, own, jnp.where(field == 6, 1.0, 0.0)))
    group = lax.shift_right_logical(iota((8, 128), 1), jnp.int32(5))
    flip = jnp.zeros((8, 128), F32)
    for s in range(4):
        flip = jnp.where(group == s, fls[s][64:72], flip)
    return jnp.concatenate(choose, axis=0), jnp.concatenate(rows, axis=0).astype(BF16), flip


def tiles_b(buf, choose):
    flat = buf.reshape(128, 128)
    turned = jnp.concatenate([flat] + [roll(flat, 32 * t, 1) for t in (1, 2, 3)], axis=0)
    got = pick(choose, turned)
    group = lax.shift_right_logical(iota((64, 128), 1), jnp.int32(5))
    out = jnp.where(group == 0, got[:64], 0.0)
    for s in (1, 2, 3):
        out = jnp.where(group == s, got[64 * s : 64 * s + 64], out)
    row = iota((8, 128), 0)
    plane = jnp.where(row >= 6, jnp.sum(buf, axis=0), 0.0)
    return out.reshape(8, 8, 128) + plane[None]


def graph(nb):
    row = iota((SUBS, SUBS), 0)
    total = jnp.zeros((SUBS, SUBS), F32)
    for s in range(4):
        total = total + (row == nb[s : s + 1]).astype(F32)
    return total


def start_inverse(g32):
    coef, const, rho = polynomial()
    g = g32.astype(BF16)
    g2 = dot(g, g)
    g2b = g2.astype(BF16)
    g3 = dot(g2b, g)
    g4 = dot(g2b, g2b)
    g3b, g4b = g3.astype(BF16), g4.astype(BF16)
    eye = (iota((SUBS, SUBS), 0) == iota((SUBS, SUBS), 1)).astype(F32)
    x = coef[0] * eye + const + coef[1] * g32 + coef[2] * g2 + coef[3] * g3 + coef[4] * g4
    x = x + coef[5] * dot(g4b, g) + coef[6] * dot(g4b, g2b) + coef[7] * dot(g4b, g3b)
    return x, rho


def newton(x, g, rho, last):
    xs = split(x, 3)
    gx = dot(g, xs[0]) + (dot(g, xs[1]) + dot(g, xs[2]))
    ones = (SIGMA / SUBS) * jnp.sum(x, axis=0, keepdims=True)
    eye = (iota((SUBS, SUBS), 0) == iota((SUBS, SUBS), 1)).astype(F32)
    rest = eye - ((128.0 + SHIFT) * x - 32.0 * gx + ones)
    x = x + mm3(xs[:2], split(rest, 2))
    if last:
        return x, 0.0
    scale = 2.0 / (2.0 - rho * rho)
    return scale * x, rho * rho / (2.0 - rho * rho)


def to_vectors(slots, c):
    wide = spread(slots, c["cmp"])
    rows = []
    for k in range(slots.shape[0] // 8):
        row, lane = iota((8, SUBS), 0), iota((8, SUBS), 1)
        keep = (lane >= row * 48) & (lane < row * 48 + 48)
        rows.append(jnp.sum(jnp.where(keep, wide[8 * k : 8 * k + 8], 0.0), axis=0, keepdims=True))
    return rows


def inverse_rows(first, xh, xl, mass):
    delta = mass - SHIFT

    def apply(d, fine):
        e = d * delta
        eh, el = split(e, 2)
        if fine:
            return d + (dot(eh, xh) + (dot(el, xh) + dot(eh, xl)))
        return d + dot(eh, xh)

    sig = 1.0 / RHO
    rk = 1.0 / sig
    rest = first
    d = rest
    y = d
    for k in range(CHEB):
        rest = rest - apply(d, k < 4)
        nxt = 1.0 / (2.0 * sig - rk)
        d = (nxt * rk) * d + (2.0 * nxt / RHO) * rest
        y = y + d
        rk = nxt
    u = y[38:39]
    t = jnp.sum(u, axis=1, keepdims=True)
    w = jnp.sum(y, axis=1, keepdims=True)
    share = (SIGMA / SUBS) / (1.0 - (SIGMA / SUBS) * t)
    return y + (w * share) * u


def coarse_parts(y, s0, s1):
    row = iota((8, SUBS), 0)
    s = jnp.where(row < EACH, s0, s1)
    group = lax.shift_right_logical(iota((8, 128), 1), jnp.int32(5))
    edges = jnp.zeros((8, 128), F32)
    for k in range(4):
        edges = jnp.where(group == k, jnp.sum(y[8 * k : 8 * k + 8] * s, axis=1, keepdims=True), edges)
    own = jnp.sum(y[32:40] * s, axis=1, keepdims=True)
    at = (iota((8, 128), 1) < SIDE) & (iota((8, 128), 0) < 6)
    return edges, jnp.where(at, own, 0.0)


def finish(r, local, mass, rims, flip, y, s0, s1, c):
    turned = spread(rims, c["rev"])
    rims = jnp.where(flip > 0.5, turned, rims)
    edges, own = coarse_parts(y, s0, s1)
    e = jnp.where(iota((8, 128), 0) < 6, edges - rims, 0.0)
    lane = iota((8, 128), 1)
    left = roll(e, 33, 1)
    both = jnp.where((lane >= 1) & (lane < 32), left, jnp.where((lane >= 32) & (lane < 64), e, 0.0))
    f, fr, fm = by_row(local), by_row(r), by_row(mass)
    z, image = [], []
    for i in range(SIDE):
        zi = f[i] + own
        moved = roll(both, 127 - i, 1)
        if i == 31:
            moved = jnp.where(lane == 0, roll(left, 96, 1), moved)
        extra = jnp.where((lane == 0) | (lane == 31), moved, 0.0)
        if i == 0:
            extra = extra + jnp.where(lane < SIDE, e, 0.0)
        if i == 31:
            extra = extra + jnp.where(lane < SIDE, roll(e, 64, 1), 0.0)
        z.append(zi)
        image.append(fr[i] + fm[i] * zi + extra)
    return jnp.concatenate(z, axis=0), jnp.concatenate(image, axis=0)


def dots_row(pairs):
    lane, row = iota((8, 128), 1), iota((8, 128), 0)
    total = jnp.zeros((8, 128), F32)
    for k, (a, b) in enumerate(pairs):
        one = jnp.sum(jnp.sum(by_row(a * b), axis=0), axis=1, keepdims=True)
        at = ((lane == k) & (row < EACH)) | ((lane == 6 + k) & (row >= EACH) & (row < 6))
        total = jnp.where(at, one, total)
    return jnp.sum(total, axis=0, keepdims=True)


def steps(row, p):
    ga, de, rw, qw, zv, wv = [row[:, 6 * p + k : 6 * p + k + 1] for k in range(6)]
    a0 = ga / de
    g1 = ga - a0 * (de + rw) + a0 * a0 * qw
    d1 = de - a0 * (qw + zv) + a0 * a0 * wv
    beta = g1 / ga
    cross = de - a0 * (0.5 * (qw + zv))
    den = d1 + 2.0 * beta * cross + beta * beta * de
    a1 = g1 / den
    return a0 + a1 * (1.0 + beta), a1 * a0


def kernel(src_hbm, mass_hbm, nb_hbm, ns_hbm, fl_hbm, s8_hbm, small_hbm, wide_hbm, inv_hbm, sol_hbm, res_hbm,
           src_v, mass_v, nb_v, ns_v, fl_v, s8_v, small_v, wide_v, inv_v,
           r_v, m_v, l_v, choose_v, e0_v, flip_v, x_v, g_v, xh_v, xl_v, first_v,
           stga0, stga1, bufa0, bufa1, stgb0, stgb1, bufb0, bufb1, st3a, st3b, buf3a, buf3b,
           out_v, insem, outsem, ssem, rsem):
    t = lax.axis_index("tile")
    lev = lax.axis_index("lev")
    plane, q = t // PLANE, t % PLANE
    line, x_at = q // LINE, q % LINE
    ready = t >= 0

    def at(dy, dz, dx, dl):
        where = ((plane + dy) % COLUMN * LINE + (line + dz) % LINE) * LINE + (x_at + dx) % LINE
        return (where, (lev + dl) % LEVS)

    a_peers = [(0, dz, dx, 0) for dz in (3, 2, 1, 0) for dx in (2, 1, 3, 0) if dz or dx]
    b_peers = [(dy, 0, 0, 0) for dy in (4, 3, 5, 2, 6, 1, 7)]
    xy_peers = [(dy, 0, dx, 0) for dy in (4, 3, 5, 2, 6, 1, 7, 0) for dx in (2, 1, 3, 0) if dy or dx]
    zc_peers = [(0, dz, 0, dl) for dz in (3, 2, 1, 0) for dl in range(LEVS) if dz or dl]
    everyone = list(dict.fromkeys(xy_peers + zc_peers + a_peers))

    moves = [(src_hbm.at[p, n], src_v.at[pl.ds(p * EACH + n, 1)]) for p in range(2) for n in range(EACH)]
    moves += [(mass_hbm, mass_v), (s8_hbm, s8_v), (small_hbm, small_v), (inv_hbm, inv_v),
              (nb_hbm, nb_v), (ns_hbm, ns_v), (fl_hbm, fl_v), (wide_hbm, wide_v)]
    copies = [pltpu.make_async_copy(a, b, insem.at[k]) for k, (a, b) in enumerate(moves)]
    for copy in copies:
        copy.start()

    barrier = pltpu.get_barrier_semaphore()
    for peer in everyone:
        pl.semaphore_signal(barrier, 1, device_id=at(*peer), device_id_type=pl.DeviceIdType.MESH)

    for copy in copies:
        copy.wait()

    def send(peers, src_of, dst, n):
        for peer in peers:
            pltpu.make_async_remote_copy(
                src_ref=src_of(peer), dst_ref=dst, send_sem=ssem.at[n], recv_sem=rsem.at[n],
                device_id=at(*peer), device_id_type=pl.DeviceIdType.MESH,
            ).start()

    def done(peers, buf, n, recv):
        view = buf.at[pl.ds(0, len(peers))]
        copy = pltpu.make_async_remote_copy(
            src_ref=view, dst_ref=view, send_sem=ssem.at[n], recv_sem=rsem.at[n],
            device_id=at(*peers[0]), device_id_type=pl.DeviceIdType.MESH,
        )
        if recv:
            copy.wait_recv()
        else:
            copy.wait_send()

    def consts():
        return {
            "s8": (s8_v[:256], s8_v[256:]),
            "s": (small_v[:SIDE], small_v[SIDE : 2 * SIDE]),
            "rev": small_v[2 * SIDE :],
            "inv": inv_v[...],
            "cmp": wide_v[...],
        }

    c = consts()
    zrow = jnp.zeros((1, 128), F32)

    first = src_v[...]
    r = to_field(jnp.where(iota(first.shape, 0) < 6, first, 0.0))
    mass = to_field(stack_fields(mass_v[...], mass_v[...]))
    r_v[...] = r
    m_v[...] = mass
    l0, rims = local_part(r, c)
    l_v[...] = l0
    tile = tile_a(rims, packed(r, q), packed(mass, q))
    stga0[...] = tile
    bufa0[q] = tile
    pl.semaphore_wait(barrier, len(everyone))
    send(a_peers, lambda peer: stga0, bufa0.at[q], 0)

    polys = polynomial()[2]
    rhos = [polys]
    for _ in range(2):
        rhos.append(rhos[-1] ** 2 / (2.0 - rhos[-1] ** 2))

    @pl.when(ready)
    def _():
        choose, e0, flip = tables(nb_v[...], ns_v[...], fl_v[...], t)
        choose_v[...] = choose
        e0_v[...] = e0
        flip_v[...] = flip
        g32 = graph(nb_v[...])
        g_v[...] = g32.astype(BF16)
        x_v[...] = start_inverse(g32)[0]

    @pl.when(ready)
    def _():
        x_v[...] = newton(x_v[...], g_v[...], rhos[0], False)[0]

    done(a_peers, bufa0, 0, True)
    stgb0[...] = tiles_b(bufa0[...], choose_v[...])
    bufb0[plane] = stgb0[plane]
    send(b_peers, lambda peer: stgb0.at[(plane + peer[0]) % COLUMN], bufb0.at[plane], 1)

    @pl.when(ready)
    def _():
        x_v[...] = newton(x_v[...], g_v[...], rhos[1], False)[0]

    @pl.when(ready)
    def _():
        x = newton(x_v[...], g_v[...], rhos[2], True)[0]
        xs = split(x, 3)
        e0 = e0_v[...]
        first_v[...] = dot(e0, xs[0]) + (dot(e0, xs[1]) + dot(e0, xs[2]))
        xh_v[...] = xs[0]
        xl_v[...] = xs[1]

    done(b_peers, bufb0, 1, True)
    c = consts()
    flip = flip_v[...]
    r, mass = r_v[...], m_v[...]
    sums = bufb0[:, 6, :]
    three = jnp.concatenate([bufb0[:, 7, :], sums, roll(sums, 128 - EACH, 1)], axis=0)
    dvec, s0, s1 = to_vectors(three, c)
    y = inverse_rows(first_v[...], xh_v[...], xl_v[...], dvec)
    z0, q0 = finish(r, l_v[...], mass, jnp.sum(bufb0[...], axis=0), flip, y, s0, s1, c)

    l1, rims = local_part(q0, c)
    tile = tile_a(rims, packed(q0, q), zrow)
    stga1[...] = tile
    bufa1[q] = tile
    send(a_peers, lambda peer: stga1, bufa1.at[q], 2)
    done(a_peers, bufa1, 2, True)
    stgb1[...] = tiles_b(bufa1[...], choose_v[...])
    bufb1[plane] = stgb1[plane]
    send(b_peers, lambda peer: stgb1.at[(plane + peer[0]) % COLUMN], bufb1.at[plane], 3)
    done(b_peers, bufb1, 3, True)
    sums = bufb1[:, 6, :]
    s0, s1 = to_vectors(jnp.concatenate([sums, roll(sums, 128 - EACH, 1)], axis=0), c)
    w, v = finish(q0, l1, mass, jnp.sum(bufb1[...], axis=0), flip, y, s0, s1, c)

    row = dots_row(((r, z0), (z0, q0), (r, w), (q0, w), (z0, v), (w, v)))
    for n, (peers, me, stg, buf) in enumerate(
        ((xy_peers, plane * LINE + x_at, st3a, buf3a), (zc_peers, line * LEVS + lev, st3b, buf3b))
    ):
        stg[...] = row
        buf[me] = row
        send(peers, lambda peer: stg, buf.at[me], 4 + n)
        done(peers, buf, 4 + n, True)
        row = jnp.sum(buf[...], axis=0)

    upper = iota((8, 128), 0) < EACH
    a0, b0 = steps(row, 0)
    a1, b1 = steps(row, 1)
    a, b = jnp.where(upper, a0, a1), jnp.where(upper, b0, b1)
    outs = [
        from_field(a[None] * by_row(z0) - b[None] * by_row(w)),
        from_field(by_row(r) - a[None] * by_row(q0) + b[None] * by_row(v)),
    ]
    last = []
    for k, (out, dst) in enumerate(zip(outs, (sol_hbm, res_hbm))):
        out_v[k] = out
        for p in range(2):
            for n in range(EACH):
                last.append(pltpu.make_async_copy(
                    out_v.at[k, pl.ds(p * EACH + n, 1)], dst.at[p, n], outsem.at[len(last)]))
    for copy in last:
        copy.start()
    for copy in last:
        copy.wait()

    done(a_peers, bufa0, 0, False)
    done(b_peers, bufb0, 1, False)
    done(a_peers, bufa1, 2, False)
    done(b_peers, bufb1, 3, False)
    done(xy_peers, buf3a, 4, False)
    done(zc_peers, buf3b, 5, False)


def shards(sources, mass_coef, neighbour_sub, neighbour_side, side_flip):
    s8, small, wide, inv = [jnp.asarray(a) for a in constants()]
    hbm = pl.BlockSpec(memory_space=pltpu.HBM)
    rows = sources.transpose(0, 2, 1, 3)
    args = [rows, mass_coef, neighbour_sub.T, neighbour_side.T, side_flip.T, s8, small, wide, inv]
    one = pltpu.VMEM((8, 128), F32)
    line = pltpu.VMEM((1, 128), F32)
    field = pltpu.VMEM((ROWS, 128), F32)
    square = lambda kind: pltpu.VMEM((SUBS, SUBS), kind)
    plane = pltpu.VMEM((PLANE, 8, 128), F32)
    column = pltpu.VMEM((COLUMN, 8, 128), F32)
    scratch = [pltpu.VMEM((8, SIDE * SIDE), F32)] + [pltpu.VMEM(a.shape, a.dtype) for a in args[1:]] + [
        field, field, field, pltpu.VMEM((256, 512), BF16), pltpu.VMEM((40, SUBS), BF16), one,
        square(F32), square(BF16), square(BF16), square(BF16), pltpu.VMEM((40, SUBS), F32),
        one, one, plane, plane, column, column, column, column, line, line,
        pltpu.VMEM((COLUMN * LINE, 1, 128), F32), pltpu.VMEM((LINE * LEVS, 1, 128), F32),
        pltpu.VMEM((2, 8, SIDE * SIDE), F32), pltpu.SemaphoreType.DMA((14,)), pltpu.SemaphoreType.DMA((12,)),
        pltpu.SemaphoreType.DMA((6,)), pltpu.SemaphoreType.DMA((6,)),
    ]
    out = jax.ShapeDtypeStruct(rows.shape, F32)
    sol, res = pl.pallas_call(
        kernel,
        out_shape=(out, out),
        in_specs=[hbm] * len(args),
        out_specs=(hbm, hbm),
        scratch_shapes=scratch,
        compiler_params=pltpu.CompilerParams(collective_id=0, has_side_effects=True, vmem_limit_bytes=67043328),
        name="schwarz",
    )(*args)
    return sol.transpose(0, 2, 1, 3), res.transpose(0, 2, 1, 3)


def solution(mesh):
    placed = (P(None, "lev", "tile", None), P("tile", None), P(), P(), P())
    return jax.shard_map(
        shards,
        mesh=mesh,
        in_specs=placed,
        out_specs=(P(None, "lev", "tile", None), P(None, "lev", "tile", None)),
        check_vma=False,
    )
```

time: 70.7 us -> 60 us (0.85)
  Pallas kernels: 63.3 us -> 57.2 us
  local copies, waits for them, and re-layouts: 5.2 us -> 1.96 us
  other arithmetic: 1.05 us -> 0 us
    pallas_call x1, Pallas kernels: 63.3 us -> 57.2 us  [shards(): pl.pallas_call(kernel, out_shape=(out, out), in_specs=[hbm] * len(args),...]
    reshape x10 -> x0, local copies, waits for them, and re-layouts: 2.37 us -> none  [the longest x2 1.43 us: shards(): return (sol.reshape(sources.shape), res.reshape(sources.shape))]
    convert_element_type x1 -> x0, other arithmetic: 0.77 us -> none  [tables(): myflip = lax.dynamic_slice_in_dim(side_flip, t * EACH, EACH, 0).astype(F32)]
    unnamed x41 -> x4, local copies, waits for them, and re-layouts: 2.21 us -> 1.96 us
where the time goes in v2:
time: 60 us; the launch traced here: 59.8 us
  Pallas kernels  57.2 us (95%)
  local copies, waits for them, and re-layouts  1.96 us (3%)
  between operations  0.65 us (1%)
    pallas_call x1, Pallas kernels, shards(): pl.pallas_call(kernel, out_shape=(out, out), in_specs=[hbm] * len(args),...  57.2 us
    unnamed x4, local copies, waits for them, and re-layouts  1.96 us

profile of v2, /device:TPU:1, one launch (start us, length us, event | category | flops | bytes accessed | tf_op | source)
XLA Modules:
  0.0 59.8 jit_solution(12596893620502912851)
XLA Ops:
  0.6 57.2 %schwarz.1 = (f32[2,3,1,1024]{3,2,1,0:T(1,128)}, f32[2,3,1,1024]{3,2,1,0:T(1,128)}) custom-call(f32[2,3,1,1024]{3,2,1,0:T(1,128)} %bitcast.6, f32[3,1024]{1,0:T(4,128)} %mass_hbm.1, s32[4,384]{1,0:T(4,128)} %bitcast.9, s32[4,384]{1,0:T(4,128)} %bitcast.10, s32[4,384]{1,0:T(4,128)} %bitcast.11, bf16[512,256]{1,0:T(8,128)(2,1)} %constant.8.clone.s8_hbm, ...), custom_call_target="tpu_custom_call" | custom-call | tf_op jit(solution)/shard_map/schwarz/pallas_call | solution.py:553
  57.8 0.0 copy-start
  57.8 1.4 %copy.13 = f32[2,1,3,1024]{3,1,2,0:T(1,128)} copy(f32[2,1,3,1024]{3,1,2,0:T(1,128)} %bitcast.8) | data formatting | bytes 49152
  59.2 0.0 copy-done
  59.2 0.6 %copy.14 = f32[2,1,3,1024]{3,1,2,0:T(1,128)} copy(f32[2,1,3,1024]{3,1,2,0:T(1,128)S(1)} %bitcast.7) | data formatting | bytes 49152
Async XLA Ops:
  57.8 1.4 %copy-start = (f32[2,3,1,1024]{3,2,1,0:T(1,128)S(1)}, f32[2,3,1,1024]{3,2,1,0:T(1,128)}, u32[]{:S(2)}) copy-start(f32[2,3,1,1024]{3,2,1,0:T(1,128)} %get-tuple-element.5) | copy-start | bytes 73732

commit v3 on v2

--- a/solution.py
+++ b/solution.py
@@ -24,7 +24,7 @@
 LOW = 32.0 * 0.06486 + SHIFT
 TOP = 32.0 * 8.0 + SHIFT
 RHO = 0.7681 / LOW
-CHEB = 7
+CHEB = 6
 
 
 def roll(x, shift, axis):
@@ -48,14 +48,14 @@
     return parts
 
 
-def pick(onehot, x):
-    a, b, c = split(x, 3)
-    return dot(onehot, a) + dot(onehot, b) + dot(onehot, c)
+def stack(parts):
+    return jnp.concatenate([part.astype(F32) for part in parts], axis=0).astype(BF16)
 
 
 def spread(x, onehot):
-    a, b, c = split(x, 3)
-    return dot(a, onehot) + dot(b, onehot) + dot(c, onehot)
+    n = x.shape[0]
+    out = dot(stack(split(x, 3)), onehot)
+    return out[:n] + out[n : 2 * n] + out[2 * n :]
 
 
 def mm3(a, b):
@@ -103,7 +103,7 @@
     lanes = np.arange(128)
     side, kk = lanes // SIDE, lanes % SIDE
     m = np.arange(SUBS)
-    cmp = ((lanes // 8)[:, None] == (m // EACH % PLANE)[None]) & ((lanes % 8)[:, None] == (m % EACH)[None])
+    cmp = ((lanes // 8)[:, None] == (m // EACH // PLANE)[None]) & ((lanes % 8)[:, None] == (m % EACH)[None])
     rev = (side[:, None] == side[None]) & (kk[:, None] == 31 - kk[None])
     s8 = np.concatenate(np_split(np.kron(sine, np.eye(8))), axis=0)
     s = np.concatenate([np.pad(a, ((0, 0), (0, 128 - SIDE))) for a in np_split(sine)], axis=0)
@@ -158,9 +158,9 @@
     return v, rims
 
 
-def packed(v, q):
+def packed(v, place):
     total = jnp.sum(jnp.sum(by_row(v), axis=0), axis=1, keepdims=True)
-    at = iota((8, 128), 1) == q * 8 + iota((8, 128), 0)
+    at = iota((8, 128), 1) == place * 8 + iota((8, 128), 0)
     return jnp.sum(jnp.where(at, total, 0.0), axis=0, keepdims=True)
 
 
@@ -171,10 +171,10 @@
 
 def tables(nb, ns, fl, t):
     plane, q = t // PLANE, t % PLANE
-    row, lane = iota((72, SUBS), 0), iota((72, SUBS), 1)
-    y = jnp.where(row < 64, lax.shift_right_logical(row, jnp.int32(3)), plane)
+    row, lane = iota((136, SUBS), 0), iota((136, SUBS), 1)
+    target = jnp.where(row < 128, lax.shift_right_logical(row, jnp.int32(3)), q)
     field = row & 7
-    sub = (y * PLANE + q) * EACH + jnp.where(field >= EACH, field - EACH, field)
+    sub = (plane * PLANE + target) * EACH + jnp.where(field >= EACH, field - EACH, field)
     take = (lane == sub) & (field < 6)
 
     def column(a, s):
@@ -184,41 +184,43 @@
     nss = [column(ns, s).astype(jnp.int32) for s in range(4)]
     fls = [column(fl, s) for s in range(4)]
 
-    field = iota((64, 1), 0) & 7
+    field = iota((128, 1), 0) & 7
     third = jnp.where(field >= EACH, EACH, 0)
-    cols = iota((64, 512), 1)
+    cols = iota((128, 256), 1)
     choose = []
     for s in range(4):
-        sub = nbs[s][:64]
+        sub = nbs[s][:128]
         device = lax.shift_right_logical(sub * 21846, jnp.int32(16))
-        at = ((s - nss[s][:64]) & 3) * 128 + (device & 15) * 8 + (sub - EACH * device) + third
-        inside = (lax.shift_right_logical(device, jnp.int32(4)) == plane) & (field < 6)
+        at = ((s - nss[s][:128]) & 3) * 64 + lax.shift_right_logical(device, jnp.int32(4)) * 8 + (sub - EACH * device) + third
+        inside = ((device & 15) == q) & (field < 6)
         choose.append((cols == jnp.where(inside, at, -1)).astype(F32).astype(BF16))
 
     field, lane = iota((8, SUBS), 0), iota((8, SUBS), 1)
     own = (lane == t * EACH + jnp.where(field >= EACH, field - EACH, field)).astype(F32)
     rows = []
     for s in range(4):
-        rows.append(jnp.where(field < 6, own - (lane == nbs[s][64:72]).astype(F32), 0.0))
+        rows.append(jnp.where(field < 6, own - (lane == nbs[s][128:136]).astype(F32), 0.0))
     rows.append(jnp.where(field < 6, own, jnp.where(field == 6, 1.0, 0.0)))
     group = lax.shift_right_logical(iota((8, 128), 1), jnp.int32(5))
     flip = jnp.zeros((8, 128), F32)
     for s in range(4):
-        flip = jnp.where(group == s, fls[s][64:72], flip)
+        flip = jnp.where(group == s, fls[s][128:136], flip)
     return jnp.concatenate(choose, axis=0), jnp.concatenate(rows, axis=0).astype(BF16), flip
 
 
 def tiles_b(buf, choose):
-    flat = buf.reshape(128, 128)
+    flat = buf.reshape(64, 128)
     turned = jnp.concatenate([flat] + [roll(flat, 32 * t, 1) for t in (1, 2, 3)], axis=0)
-    got = pick(choose, turned)
-    group = lax.shift_right_logical(iota((64, 128), 1), jnp.int32(5))
-    out = jnp.where(group == 0, got[:64], 0.0)
+    a, b, c = split(turned, 3)
+    wide = dot(choose, jnp.concatenate([a, b], axis=1))
+    got = (wide[:, :128] + wide[:, 128:]) + dot(choose, c)
+    group = lax.shift_right_logical(iota((128, 128), 1), jnp.int32(5))
+    out = jnp.where(group == 0, got[:128], 0.0)
     for s in (1, 2, 3):
-        out = jnp.where(group == s, got[64 * s : 64 * s + 64], out)
+        out = jnp.where(group == s, got[128 * s : 128 * s + 128], out)
     row = iota((8, 128), 0)
-    plane = jnp.where(row >= 6, jnp.sum(buf, axis=0), 0.0)
-    return out.reshape(8, 8, 128) + plane[None]
+    column = jnp.where(row >= 6, jnp.sum(buf, axis=0), 0.0)
+    return out.reshape(PLANE, 8, 128) + column[None]
 
 
 def graph(nb):
@@ -258,11 +260,12 @@
 
 def to_vectors(slots, c):
     wide = spread(slots, c["cmp"])
+    row, lane = iota((PLANE, SUBS), 0), iota((PLANE, SUBS), 1)
+    keep = (lax.shift_right_logical(lane * 21846, jnp.int32(16)) & 15) == row
     rows = []
-    for k in range(slots.shape[0] // 8):
-        row, lane = iota((8, SUBS), 0), iota((8, SUBS), 1)
-        keep = (lane >= row * 48) & (lane < row * 48 + 48)
-        rows.append(jnp.sum(jnp.where(keep, wide[8 * k : 8 * k + 8], 0.0), axis=0, keepdims=True))
+    for k in range(slots.shape[0] // PLANE):
+        block = wide[PLANE * k : PLANE * k + PLANE]
+        rows.append(jnp.sum(jnp.where(keep, block, 0.0), axis=0, keepdims=True))
     return rows
 
 
@@ -271,10 +274,12 @@
 
     def apply(d, fine):
         e = d * delta
+        if not fine:
+            return d + dot(e.astype(BF16), xh)
         eh, el = split(e, 2)
-        if fine:
-            return d + (dot(eh, xh) + (dot(el, xh) + dot(eh, xl)))
-        return d + dot(eh, xh)
+        n = e.shape[0]
+        high = dot(stack([eh, el]), xh)
+        return d + (high[:n] + (high[n:] + dot(eh, xl)))
 
     sig = 1.0 / RHO
     rk = 1.0 / sig
@@ -282,7 +287,7 @@
     d = rest
     y = d
     for k in range(CHEB):
-        rest = rest - apply(d, k < 4)
+        rest = rest - apply(d, k < 3)
         nxt = 1.0 / (2.0 * sig - rk)
         d = (nxt * rk) * d + (2.0 * nxt / RHO) * rest
         y = y + d
@@ -353,11 +358,11 @@
     return a0 + a1 * (1.0 + beta), a1 * a0
 
 
-def kernel(src_hbm, mass_hbm, nb_hbm, ns_hbm, fl_hbm, s8_hbm, small_hbm, wide_hbm, inv_hbm, sol_hbm, res_hbm,
+def kernel(src_hbm, mass_hbm, nb_hbm, ns_hbm, fl_hbm, s8_hbm, small_hbm, wide_hbm, inv_hbm, out_hbm,
            src_v, mass_v, nb_v, ns_v, fl_v, s8_v, small_v, wide_v, inv_v,
            r_v, m_v, l_v, choose_v, e0_v, flip_v, x_v, g_v, xh_v, xl_v, first_v,
            stga0, stga1, bufa0, bufa1, stgb0, stgb1, bufb0, bufb1, st3a, st3b, buf3a, buf3b,
-           out_v, insem, outsem, ssem, rsem):
+           out_v, nat_v, insem, outsem, ssem, rsem):
     t = lax.axis_index("tile")
     lev = lax.axis_index("lev")
     plane, q = t // PLANE, t % PLANE
@@ -368,11 +373,11 @@
         where = ((plane + dy) % COLUMN * LINE + (line + dz) % LINE) * LINE + (x_at + dx) % LINE
         return (where, (lev + dl) % LEVS)
 
-    a_peers = [(0, dz, dx, 0) for dz in (3, 2, 1, 0) for dx in (2, 1, 3, 0) if dz or dx]
-    b_peers = [(dy, 0, 0, 0) for dy in (4, 3, 5, 2, 6, 1, 7)]
+    a_peers = [(dy, 0, 0, 0) for dy in (4, 3, 5, 2, 6, 1, 7)]
+    b_peers = [(0, dz, dx, 0) for dz in (3, 2, 1, 0) for dx in (2, 1, 3, 0) if dz or dx]
     xy_peers = [(dy, 0, dx, 0) for dy in (4, 3, 5, 2, 6, 1, 7, 0) for dx in (2, 1, 3, 0) if dy or dx]
     zc_peers = [(0, dz, 0, dl) for dz in (3, 2, 1, 0) for dl in range(LEVS) if dz or dl]
-    everyone = list(dict.fromkeys(xy_peers + zc_peers + a_peers))
+    everyone = list(dict.fromkeys(a_peers + b_peers + xy_peers + zc_peers))
 
     moves = [(src_hbm.at[p, n], src_v.at[pl.ds(p * EACH + n, 1)]) for p in range(2) for n in range(EACH)]
     moves += [(mass_hbm, mass_v), (s8_hbm, s8_v), (small_hbm, small_v), (inv_hbm, inv_v),
@@ -387,6 +392,9 @@
 
     for copy in copies:
         copy.wait()
+
+    def spot(peer):
+        return (line + peer[1]) % LINE * LINE + (x_at + peer[2]) % LINE
 
     def send(peers, src_of, dst, n):
         for peer in peers:
@@ -425,11 +433,11 @@
     m_v[...] = mass
     l0, rims = local_part(r, c)
     l_v[...] = l0
-    tile = tile_a(rims, packed(r, q), packed(mass, q))
+    tile = tile_a(rims, packed(r, plane), packed(mass, plane))
     stga0[...] = tile
-    bufa0[q] = tile
+    bufa0[plane] = tile
     pl.semaphore_wait(barrier, len(everyone))
-    send(a_peers, lambda peer: stga0, bufa0.at[q], 0)
+    send(a_peers, lambda peer: stga0, bufa0.at[plane], 0)
 
     polys = polynomial()[2]
     rhos = [polys]
@@ -452,8 +460,8 @@
 
     done(a_peers, bufa0, 0, True)
     stgb0[...] = tiles_b(bufa0[...], choose_v[...])
-    bufb0[plane] = stgb0[plane]
-    send(b_peers, lambda peer: stgb0.at[(plane + peer[0]) % COLUMN], bufb0.at[plane], 1)
+    bufb0[q] = stgb0[q]
+    send(b_peers, lambda peer: stgb0.at[spot(peer)], bufb0.at[q], 1)
 
     @pl.when(ready)
     def _():
@@ -479,39 +487,44 @@
     z0, q0 = finish(r, l_v[...], mass, jnp.sum(bufb0[...], axis=0), flip, y, s0, s1, c)
 
     l1, rims = local_part(q0, c)
-    tile = tile_a(rims, packed(q0, q), zrow)
+    tile = tile_a(rims, packed(q0, plane), zrow)
     stga1[...] = tile
-    bufa1[q] = tile
-    send(a_peers, lambda peer: stga1, bufa1.at[q], 2)
+    bufa1[plane] = tile
+    send(a_peers, lambda peer: stga1, bufa1.at[plane], 2)
     done(a_peers, bufa1, 2, True)
     stgb1[...] = tiles_b(bufa1[...], choose_v[...])
-    bufb1[plane] = stgb1[plane]
-    send(b_peers, lambda peer: stgb1.at[(plane + peer[0]) % COLUMN], bufb1.at[plane], 3)
+    bufb1[q] = stgb1[q]
+    send(b_peers, lambda peer: stgb1.at[spot(peer)], bufb1.at[q], 3)
     done(b_peers, bufb1, 3, True)
     sums = bufb1[:, 6, :]
     s0, s1 = to_vectors(jnp.concatenate([sums, roll(sums, 128 - EACH, 1)], axis=0), c)
     w, v = finish(q0, l1, mass, jnp.sum(bufb1[...], axis=0), flip, y, s0, s1, c)
 
     row = dots_row(((r, z0), (z0, q0), (r, w), (q0, w), (z0, v), (w, v)))
-    for n, (peers, me, stg, buf) in enumerate(
-        ((xy_peers, plane * LINE + x_at, st3a, buf3a), (zc_peers, line * LEVS + lev, st3b, buf3b))
-    ):
-        stg[...] = row
-        buf[me] = row
-        send(peers, lambda peer: stg, buf.at[me], 4 + n)
-        done(peers, buf, 4 + n, True)
-        row = jnp.sum(buf[...], axis=0)
-
-    upper = iota((8, 128), 0) < EACH
+    st3a[...] = row
+    buf3a[plane * LINE + x_at] = row
+    send(xy_peers, lambda peer: st3a, buf3a.at[plane * LINE + x_at], 4)
+
+    @pl.when(ready)
+    def _():
+        for k, field in enumerate((z0, q0, w, v)):
+            nat_v[k] = from_field(by_row(field))
+
+    done(xy_peers, buf3a, 4, True)
+    row = jnp.sum(buf3a[...], axis=0)
+    st3b[...] = row
+    buf3b[line * LEVS + lev] = row
+    send(zc_peers, lambda peer: st3b, buf3b.at[line * LEVS + lev], 5)
+    done(zc_peers, buf3b, 5, True)
+    row = jnp.sum(buf3b[...], axis=0)
+
+    upper = iota((8, 1), 0) < EACH
     a0, b0 = steps(row, 0)
     a1, b1 = steps(row, 1)
     a, b = jnp.where(upper, a0, a1), jnp.where(upper, b0, b1)
-    outs = [
-        from_field(a[None] * by_row(z0) - b[None] * by_row(w)),
-        from_field(by_row(r) - a[None] * by_row(q0) + b[None] * by_row(v)),
-    ]
+    outs = [a * nat_v[0] - b * nat_v[2], src_v[...] - a * nat_v[1] + b * nat_v[3]]
     last = []
-    for k, (out, dst) in enumerate(zip(outs, (sol_hbm, res_hbm))):
+    for k, (out, dst) in enumerate(zip(outs, (out_hbm.at[0], out_hbm.at[1]))):
         out_v[k] = out
         for p in range(2):
             for n in range(EACH):
@@ -542,24 +555,25 @@
     plane = pltpu.VMEM((PLANE, 8, 128), F32)
     column = pltpu.VMEM((COLUMN, 8, 128), F32)
     scratch = [pltpu.VMEM((8, SIDE * SIDE), F32)] + [pltpu.VMEM(a.shape, a.dtype) for a in args[1:]] + [
-        field, field, field, pltpu.VMEM((256, 512), BF16), pltpu.VMEM((40, SUBS), BF16), one,
+        field, field, field, pltpu.VMEM((512, 256), BF16), pltpu.VMEM((40, SUBS), BF16), one,
         square(F32), square(BF16), square(BF16), square(BF16), pltpu.VMEM((40, SUBS), F32),
-        one, one, plane, plane, column, column, column, column, line, line,
+        one, one, column, column, plane, plane, plane, plane, line, line,
         pltpu.VMEM((COLUMN * LINE, 1, 128), F32), pltpu.VMEM((LINE * LEVS, 1, 128), F32),
-        pltpu.VMEM((2, 8, SIDE * SIDE), F32), pltpu.SemaphoreType.DMA((14,)), pltpu.SemaphoreType.DMA((12,)),
+        pltpu.VMEM((2, 8, SIDE * SIDE), F32), pltpu.VMEM((4, 8, SIDE * SIDE), F32), pltpu.SemaphoreType.DMA((14,)), pltpu.SemaphoreType.DMA((12,)),
         pltpu.SemaphoreType.DMA((6,)), pltpu.SemaphoreType.DMA((6,)),
     ]
-    out = jax.ShapeDtypeStruct(rows.shape, F32)
-    sol, res = pl.pallas_call(
+    out = jax.ShapeDtypeStruct((2,) + rows.shape, F32)
+    both = pl.pallas_call(
         kernel,
-        out_shape=(out, out),
+        out_shape=out,
         in_specs=[hbm] * len(args),
-        out_specs=(hbm, hbm),
+        out_specs=hbm,
         scratch_shapes=scratch,
         compiler_params=pltpu.CompilerParams(collective_id=0, has_side_effects=True, vmem_limit_bytes=67043328),
         name="schwarz",
     )(*args)
-    return sol.transpose(0, 2, 1, 3), res.transpose(0, 2, 1, 3)
+    both = both.transpose(0, 1, 3, 2, 4)
+    return both[0], both[1]
 
 
 def solution(mesh):

time: 60 us -> 58.6 us (0.977)
  Pallas kernels: 57.2 us -> 56.4 us
    unnamed x4 -> x0, local copies, waits for them, and re-layouts: 1.96 us -> none
    squeeze x0 -> x1, local copies, waits for them, and re-layouts: none -> 1.38 us  [shards(): return (both[0], both[1])]
    pallas_call x1, Pallas kernels: 57.2 us -> 56.4 us  [shards(): pl.pallas_call(kernel, out_shape=out, in_specs=[hbm] * len(args), out_spe...]
where the time goes in v3:
time: 58.6 us; the launch traced here: 58.4 us
  Pallas kernels  56.4 us (96%)
  local copies, waits for them, and re-layouts  1.38 us (2%)
  between operations  0.64 us (1%)
    pallas_call x1, Pallas kernels, shards(): pl.pallas_call(kernel, out_shape=out, in_specs=[hbm] * len(args), out_spe...  56.4 us
    squeeze x1, local copies, waits for them, and re-layouts, shards(): return (both[0], both[1])  1.38 us

profile of v3, /device:TPU:1, one launch (start us, length us, event | category | flops | bytes accessed | tf_op | source)
XLA Modules:
  0.0 58.4 jit_solution(1652018968722070296)
XLA Ops:
  0.6 56.4 %schwarz.1 = f32[2,2,3,1,1024]{4,3,2,1,0:T(1,128)} custom-call(f32[2,3,1,1024]{3,2,1,0:T(1,128)} %bitcast.8, f32[3,1024]{1,0:T(4,128)} %mass_hbm.1, s32[4,384]{1,0:T(4,128)} %bitcast.9, s32[4,384]{1,0:T(4,128)} %bitcast.10, s32[4,384]{1,0:T(4,128)} %bitcast.11, bf16[512,256]{1,0:T(8,128)(2,1)} %constant.8.clone.s8_hbm, ...), custom_call_target="tpu_custom_call" | custom-call | tf_op jit(solution)/shard_map/schwarz/pallas_call | solution.py:566
  57.0 1.4 %slice_bitcast_fusion = (f32[2,1,3,1024]{3,1,2,0:T(1,128)}, f32[2,1,3,1024]{3,1,2,0:T(1,128)}) fusion(f32[2,2,3,1,1024]{4,3,2,1,0:T(1,128)} %schwarz.1), kind=kLoop, calls=%fused_computation | loop fusion | bytes 98304 | tf_op jit(solution)/shard_map/squeeze | solution.py:576

commit v4 on v3

--- a/solution.py
+++ b/solution.py
@@ -107,7 +107,12 @@
     rev = (side[:, None] == side[None]) & (kk[:, None] == 31 - kk[None])
     s8 = np.concatenate(np_split(np.kron(sine, np.eye(8))), axis=0)
     s = np.concatenate([np.pad(a, ((0, 0), (0, 128 - SIDE))) for a in np_split(sine)], axis=0)
-    small = np.concatenate([s, rev.astype(np.float32).astype(jnp.bfloat16)], axis=0)
+    ends = np.zeros((SIDE, 128))
+    ends[:, 32:64] = sine[:, 31:32]
+    ends[:, 96:] = sine[:, 0:1]
+    quad = np.kron(np.eye(4), sine)
+    rev = rev.astype(np.float32).astype(jnp.bfloat16)
+    small = np.concatenate([s, *np_split(ends), *np_split(quad), rev], axis=0)
     wide = cmp.astype(np.float32).astype(jnp.bfloat16)
     return s8, small, wide, inv.astype(np.float32)
 
@@ -141,21 +146,31 @@
     return jnp.concatenate(parts, axis=1)
 
 
-def local_part(r, c):
+def coefficients(r, c):
     v = mm3(c["s8"], split(r[:, :SIDE], 2))
-    v = mm3(split(v, 2), c["s"])[:, :SIDE] * c["inv"]
-    v = mm3(split(v, 2), c["s"])
-    v = mm3(c["s8"], split(v, 2))
-    f = by_row(v)
-    lane = iota((8, 128), 1)
-    right = jnp.zeros((8, 128), F32)
-    left = jnp.zeros((8, 128), F32)
+    return mm3(split(v, 2), c["s"])[:, :SIDE] * c["inv"]
+
+
+def local_rims(x, c):
+    w = by_row(mm3(split(x, 2), c["ends"]))
+    f = x.reshape(SIDE, 8, SIDE)
+    lane = iota((8, 128), 1) & 63
+    scale = [math.sqrt(2.0 / 33.0) * math.sin(math.pi * (i + 1) / 33.0) for i in range(SIDE)]
+    even = sum(scale[i] * f[i] for i in range(0, SIDE, 2))
+    odd = sum(scale[i] * f[i] for i in range(1, SIDE, 2))
+    blank = jnp.zeros((8, SIDE), F32)
+    tile = jnp.concatenate([even + odd, blank, even - odd, blank], axis=1)
     for i in range(SIDE):
-        moved = roll(f[i], i + 1, 1)
-        right = jnp.where(lane == 32 + i, moved, right)
-        left = jnp.where(lane == 1 + i, moved, left)
-    rims = (f[0] + roll(f[31], 64, 1)) + (right + roll(left, 95, 1))
-    return v, rims
+        tile = jnp.where(lane == 32 + i, w[i], tile)
+    th, tl = split(tile, 2)
+    qh, ql = c["quad"]
+    both = dot(stack([th, tl]), qh)
+    return both[:8] + (both[8:] + dot(th, ql))
+
+
+def local_field(x, c):
+    v = mm3(split(x, 2), c["s"])
+    return mm3(c["s8"], split(v, 2))
 
 
 def packed(v, place):
@@ -311,10 +326,9 @@
     return edges, jnp.where(at, own, 0.0)
 
 
-def finish(r, local, mass, rims, flip, y, s0, s1, c):
+def finish(r, local, mass, rims, flip, edges, own, c):
     turned = spread(rims, c["rev"])
     rims = jnp.where(flip > 0.5, turned, rims)
-    edges, own = coarse_parts(y, s0, s1)
     e = jnp.where(iota((8, 128), 0) < 6, edges - rims, 0.0)
     lane = iota((8, 128), 1)
     left = roll(e, 33, 1)
@@ -362,7 +376,7 @@
            src_v, mass_v, nb_v, ns_v, fl_v, s8_v, small_v, wide_v, inv_v,
            r_v, m_v, l_v, choose_v, e0_v, flip_v, x_v, g_v, xh_v, xl_v, first_v,
            stga0, stga1, bufa0, bufa1, stgb0, stgb1, bufb0, bufb1, st3a, st3b, buf3a, buf3b,
-           out_v, nat_v, insem, outsem, ssem, rsem):
+           out_v, nat_v, stgm, bufm, y_v, edge_v, own_v, insem, outsem, ssem, rsem):
     t = lax.axis_index("tile")
     lev = lax.axis_index("lev")
     plane, q = t // PLANE, t % PLANE
@@ -418,7 +432,9 @@
         return {
             "s8": (s8_v[:256], s8_v[256:]),
             "s": (small_v[:SIDE], small_v[SIDE : 2 * SIDE]),
-            "rev": small_v[2 * SIDE :],
+            "ends": (small_v[64:96], small_v[96:128]),
+            "quad": (small_v[128:256], small_v[256:384]),
+            "rev": small_v[384:],
             "inv": inv_v[...],
             "cmp": wide_v[...],
         }
@@ -431,8 +447,8 @@
     mass = to_field(stack_fields(mass_v[...], mass_v[...]))
     r_v[...] = r
     m_v[...] = mass
-    l0, rims = local_part(r, c)
-    l_v[...] = l0
+    x0 = coefficients(r, c)
+    rims = local_rims(x0, c)
     tile = tile_a(rims, packed(r, plane), packed(mass, plane))
     stga0[...] = tile
     bufa0[plane] = tile
@@ -446,6 +462,7 @@
 
     @pl.when(ready)
     def _():
+        l_v[...] = local_field(x0, c)
         choose, e0, flip = tables(nb_v[...], ns_v[...], fl_v[...], t)
         choose_v[...] = choose
         e0_v[...] = e0
@@ -459,6 +476,10 @@
         x_v[...] = newton(x_v[...], g_v[...], rhos[0], False)[0]
 
     done(a_peers, bufa0, 0, True)
+    total = jnp.sum(bufa0[...], axis=0)[6:8]
+    stgm[...] = total
+    bufm[q] = total
+    send(b_peers, lambda peer: stgm, bufm.at[q], 6)
     stgb0[...] = tiles_b(bufa0[...], choose_v[...])
     bufb0[q] = stgb0[q]
     send(b_peers, lambda peer: stgb0.at[spot(peer)], bufb0.at[q], 1)
@@ -476,21 +497,34 @@
         xh_v[...] = xs[0]
         xl_v[...] = xs[1]
 
+    done(b_peers, bufm, 6, True)
+
+    @pl.when(ready)
+    def _():
+        sums = bufm[:, 0, :]
+        three = jnp.concatenate([bufm[:, 1, :], sums, roll(sums, 128 - EACH, 1)], axis=0)
+        dvec, s0, s1 = to_vectors(three, consts())
+        y = inverse_rows(first_v[...], xh_v[...], xl_v[...], dvec)
+        y_v[...] = y
+        edge_v[...], own_v[...] = coarse_parts(y, s0, s1)
+
     done(b_peers, bufb0, 1, True)
     c = consts()
     flip = flip_v[...]
     r, mass = r_v[...], m_v[...]
-    sums = bufb0[:, 6, :]
-    three = jnp.concatenate([bufb0[:, 7, :], sums, roll(sums, 128 - EACH, 1)], axis=0)
-    dvec, s0, s1 = to_vectors(three, c)
-    y = inverse_rows(first_v[...], xh_v[...], xl_v[...], dvec)
-    z0, q0 = finish(r, l_v[...], mass, jnp.sum(bufb0[...], axis=0), flip, y, s0, s1, c)
-
-    l1, rims = local_part(q0, c)
+    z0, q0 = finish(r, l_v[...], mass, jnp.sum(bufb0[...], axis=0), flip, edge_v[...], own_v[...], c)
+
+    x1 = coefficients(q0, c)
+    rims = local_rims(x1, c)
     tile = tile_a(rims, packed(q0, plane), zrow)
     stga1[...] = tile
     bufa1[plane] = tile
     send(a_peers, lambda peer: stga1, bufa1.at[plane], 2)
+
+    @pl.when(ready)
+    def _():
+        l_v[...] = local_field(x1, c)
+
     done(a_peers, bufa1, 2, True)
     stgb1[...] = tiles_b(bufa1[...], choose_v[...])
     bufb1[q] = stgb1[q]
@@ -498,7 +532,8 @@
     done(b_peers, bufb1, 3, True)
     sums = bufb1[:, 6, :]
     s0, s1 = to_vectors(jnp.concatenate([sums, roll(sums, 128 - EACH, 1)], axis=0), c)
-    w, v = finish(q0, l1, mass, jnp.sum(bufb1[...], axis=0), flip, y, s0, s1, c)
+    edges, own = coarse_parts(y_v[...], s0, s1)
+    w, v = finish(q0, l_v[...], mass, jnp.sum(bufb1[...], axis=0), flip, edges, own, c)
 
     row = dots_row(((r, z0), (z0, q0), (r, w), (q0, w), (z0, v), (w, v)))
     st3a[...] = row
@@ -541,6 +576,7 @@
     done(b_peers, bufb1, 3, False)
     done(xy_peers, buf3a, 4, False)
     done(zc_peers, buf3b, 5, False)
+    done(b_peers, bufm, 6, False)
 
 
 def shards(sources, mass_coef, neighbour_sub, neighbour_side, side_flip):
@@ -559,8 +595,10 @@
         square(F32), square(BF16), square(BF16), square(BF16), pltpu.VMEM((40, SUBS), F32),
         one, one, column, column, plane, plane, plane, plane, line, line,
         pltpu.VMEM((COLUMN * LINE, 1, 128), F32), pltpu.VMEM((LINE * LEVS, 1, 128), F32),
-        pltpu.VMEM((2, 8, SIDE * SIDE), F32), pltpu.VMEM((4, 8, SIDE * SIDE), F32), pltpu.SemaphoreType.DMA((14,)), pltpu.SemaphoreType.DMA((12,)),
-        pltpu.SemaphoreType.DMA((6,)), pltpu.SemaphoreType.DMA((6,)),
+        pltpu.VMEM((2, 8, SIDE * SIDE), F32), pltpu.VMEM((4, 8, SIDE * SIDE), F32),
+        pltpu.VMEM((2, 128), F32), pltpu.VMEM((PLANE, 2, 128), F32), pltpu.VMEM((40, SUBS), F32), one, one,
+        pltpu.SemaphoreType.DMA((14,)), pltpu.SemaphoreType.DMA((12,)),
+        pltpu.SemaphoreType.DMA((7,)), pltpu.SemaphoreType.DMA((7,)),
     ]
     out = jax.ShapeDtypeStruct((2,) + rows.shape, F32)
     both = pl.pallas_call(

time: 58.6 us -> 58.1 us (level)
  Pallas kernels: 56.4 us -> 55.8 us
where the time goes in v4:
time: 58.1 us; the launch traced here: 57.9 us
  Pallas kernels  55.8 us (96%)
  local copies, waits for them, and re-layouts  1.38 us (2%)
  between operations  0.64 us (1%)
    pallas_call x1, Pallas kernels, shards(): pl.pallas_call(kernel, out_shape=out, in_specs=[hbm] * len(args), out_spe...  55.8 us
    squeeze x1, local copies, waits for them, and re-layouts, shards(): return (both[0], both[1])  1.38 us

profile of v4, /device:TPU:1, one launch (start us, length us, event | category | flops | bytes accessed | tf_op | source)
XLA Modules:
  0.0 57.9 jit_solution(15939669661167887496)
XLA Ops:
  0.6 55.8 %schwarz.1 = f32[2,2,3,1,1024]{4,3,2,1,0:T(1,128)} custom-call(f32[2,3,1,1024]{3,2,1,0:T(1,128)} %bitcast.8, f32[3,1024]{1,0:T(4,128)} %mass_hbm.1, s32[4,384]{1,0:T(4,128)} %bitcast.9, s32[4,384]{1,0:T(4,128)} %bitcast.10, s32[4,384]{1,0:T(4,128)} %bitcast.11, bf16[512,256]{1,0:T(8,128)(2,1)} %constant.8.clone.s8_hbm, ...), custom_call_target="tpu_custom_call" | custom-call | tf_op jit(solution)/shard_map/schwarz/pallas_call | solution.py:604
  56.5 1.4 %slice_bitcast_fusion = (f32[2,1,3,1024]{3,1,2,0:T(1,128)}, f32[2,1,3,1024]{3,1,2,0:T(1,128)}) fusion(f32[2,2,3,1,1024]{4,3,2,1,0:T(1,128)} %schwarz.1), kind=kLoop, calls=%fused_computation | loop fusion | bytes 98304 | tf_op jit(solution)/shard_map/squeeze | solution.py:614

commit v5 on v4

--- a/solution.py
+++ b/solution.py
@@ -372,11 +372,11 @@
     return a0 + a1 * (1.0 + beta), a1 * a0
 
 
-def kernel(src_hbm, mass_hbm, nb_hbm, ns_hbm, fl_hbm, s8_hbm, small_hbm, wide_hbm, inv_hbm, out_hbm,
+def kernel(src_hbm, mass_hbm, nb_hbm, ns_hbm, fl_hbm, s8_hbm, small_hbm, wide_hbm, inv_hbm, out_ref,
            src_v, mass_v, nb_v, ns_v, fl_v, s8_v, small_v, wide_v, inv_v,
            r_v, m_v, l_v, choose_v, e0_v, flip_v, x_v, g_v, xh_v, xl_v, first_v,
            stga0, stga1, bufa0, bufa1, stgb0, stgb1, bufb0, bufb1, st3a, st3b, buf3a, buf3b,
-           out_v, nat_v, stgm, bufm, y_v, edge_v, own_v, insem, outsem, ssem, rsem):
+           nat_v, stgm, bufm, y_v, edge_v, own_v, insem, ssem, rsem, opensem):
     t = lax.axis_index("tile")
     lev = lax.axis_index("lev")
     plane, q = t // PLANE, t % PLANE
@@ -391,7 +391,8 @@
     b_peers = [(0, dz, dx, 0) for dz in (3, 2, 1, 0) for dx in (2, 1, 3, 0) if dz or dx]
     xy_peers = [(dy, 0, dx, 0) for dy in (4, 3, 5, 2, 6, 1, 7, 0) for dx in (2, 1, 3, 0) if dy or dx]
     zc_peers = [(0, dz, 0, dl) for dz in (3, 2, 1, 0) for dl in range(LEVS) if dz or dl]
-    everyone = list(dict.fromkeys(a_peers + b_peers + xy_peers + zc_peers))
+    l_peers = [(0, 0, 0, dl) for dl in (2, 3, 4, 5, 1)]
+    everyone = a_peers + b_peers + l_peers
 
     moves = [(src_hbm.at[p, n], src_v.at[pl.ds(p * EACH + n, 1)]) for p in range(2) for n in range(EACH)]
     moves += [(mass_hbm, mass_v), (s8_hbm, s8_v), (small_hbm, small_v), (inv_hbm, inv_v),
@@ -509,6 +510,8 @@
         edge_v[...], own_v[...] = coarse_parts(y, s0, s1)
 
     done(b_peers, bufb0, 1, True)
+    for peer in l_peers:
+        pl.semaphore_signal(opensem, 1, device_id=at(*peer), device_id_type=pl.DeviceIdType.MESH)
     c = consts()
     flip = flip_v[...]
     r, mass = r_v[...], m_v[...]
@@ -549,6 +552,7 @@
     row = jnp.sum(buf3a[...], axis=0)
     st3b[...] = row
     buf3b[line * LEVS + lev] = row
+    pl.semaphore_wait(opensem, len(l_peers))
     send(zc_peers, lambda peer: st3b, buf3b.at[line * LEVS + lev], 5)
     done(zc_peers, buf3b, 5, True)
     row = jnp.sum(buf3b[...], axis=0)
@@ -558,17 +562,10 @@
     a1, b1 = steps(row, 1)
     a, b = jnp.where(upper, a0, a1), jnp.where(upper, b0, b1)
     outs = [a * nat_v[0] - b * nat_v[2], src_v[...] - a * nat_v[1] + b * nat_v[3]]
-    last = []
-    for k, (out, dst) in enumerate(zip(outs, (out_hbm.at[0], out_hbm.at[1]))):
-        out_v[k] = out
+    for k, out in enumerate(outs):
         for p in range(2):
             for n in range(EACH):
-                last.append(pltpu.make_async_copy(
-                    out_v.at[k, pl.ds(p * EACH + n, 1)], dst.at[p, n], outsem.at[len(last)]))
-    for copy in last:
-        copy.start()
-    for copy in last:
-        copy.wait()
+                out_ref[k, p, n] = out[p * EACH + n : p * EACH + n + 1]
 
     done(a_peers, bufa0, 0, False)
     done(b_peers, bufb0, 1, False)
@@ -595,19 +592,19 @@
         square(F32), square(BF16), square(BF16), square(BF16), pltpu.VMEM((40, SUBS), F32),
         one, one, column, column, plane, plane, plane, plane, line, line,
         pltpu.VMEM((COLUMN * LINE, 1, 128), F32), pltpu.VMEM((LINE * LEVS, 1, 128), F32),
-        pltpu.VMEM((2, 8, SIDE * SIDE), F32), pltpu.VMEM((4, 8, SIDE * SIDE), F32),
+        pltpu.VMEM((4, 8, SIDE * SIDE), F32),
         pltpu.VMEM((2, 128), F32), pltpu.VMEM((PLANE, 2, 128), F32), pltpu.VMEM((40, SUBS), F32), one, one,
-        pltpu.SemaphoreType.DMA((14,)), pltpu.SemaphoreType.DMA((12,)),
-        pltpu.SemaphoreType.DMA((7,)), pltpu.SemaphoreType.DMA((7,)),
+        pltpu.SemaphoreType.DMA((14,)),
+        pltpu.SemaphoreType.DMA((7,)), pltpu.SemaphoreType.DMA((7,)), pltpu.SemaphoreType.REGULAR,
     ]
-    out = jax.ShapeDtypeStruct((2,) + rows.shape, F32)
+    out = pltpu.VMEM((2,) + rows.shape, F32)
     both = pl.pallas_call(
         kernel,
         out_shape=out,
         in_specs=[hbm] * len(args),
-        out_specs=hbm,
+        out_specs=pl.BlockSpec(memory_space=pltpu.VMEM),
         scratch_shapes=scratch,
-        compiler_params=pltpu.CompilerParams(collective_id=0, has_side_effects=True, vmem_limit_bytes=67043328),
+        compiler_params=pltpu.CompilerParams(collective_id=0, has_side_effects=True, vmem_limit_bytes=60 << 20),
         name="schwarz",
     )(*args)
     both = both.transpose(0, 1, 3, 2, 4)

time: 58.1 us -> 56 us (0.964)
  Pallas kernels: 55.8 us -> 54.5 us
  local copies, waits for them, and re-layouts: 1.38 us -> 0.62 us
    pallas_call x1, Pallas kernels: 55.8 us -> 54.5 us  [shards(): pl.pallas_call(kernel, out_shape=out, in_specs=[hbm] * len(args), out_spe...]
    squeeze x1, local copies, waits for them, and re-layouts: 1.38 us -> 0.62 us  [shards(): return (both[0], both[1])]
where the time goes in v5:
time: 56 us; the launch traced here: 55.8 us
  Pallas kernels  54.5 us (97%)
  between operations  0.64 us (1%)
  local copies, waits for them, and re-layouts  0.62 us (1%)
    pallas_call x1, Pallas kernels, shards(): pl.pallas_call(kernel, out_shape=out, in_specs=[hbm] * len(args), out_spe...  54.5 us

profile of v5, /device:TPU:1, one launch (start us, length us, event | category | flops | bytes accessed | tf_op | source)
XLA Modules:
  0.0 55.8 jit_solution(10757846154839066584)
XLA Ops:
  0.6 54.5 %schwarz.1 = f32[2,2,3,1,1024]{4,3,2,1,0:T(1,128)S(1)} custom-call(f32[2,3,1,1024]{3,2,1,0:T(1,128)} %bitcast.8, f32[3,1024]{1,0:T(4,128)} %mass_hbm.1, s32[4,384]{1,0:T(4,128)} %bitcast.9, s32[4,384]{1,0:T(4,128)} %bitcast.10, s32[4,384]{1,0:T(4,128)} %bitcast.11, bf16[512,256]{1,0:T(8,128)(2,1)} %constant.8.clone.s8_hbm, ...), custom_call_target="tpu_custom_call" | custom-call | tf_op jit(solution)/shard_map/schwarz/pallas_call | solution.py:601
  55.2 0.6 %slice_bitcast_fusion = (f32[2,1,3,1024]{3,1,2,0:T(1,128)}, f32[2,1,3,1024]{3,1,2,0:T(1,128)}) fusion(f32[2,2,3,1,1024]{4,3,2,1,0:T(1,128)S(1)} %schwarz.1), kind=kLoop, calls=%fused_computation | loop fusion | bytes 98304 | tf_op jit(solution)/shard_map/squeeze | solution.py:611

commit v6 on v5

--- a/solution.py
+++ b/solution.py
@@ -350,14 +350,14 @@
     return jnp.concatenate(z, axis=0), jnp.concatenate(image, axis=0)
 
 
-def dots_row(pairs):
+def dots_tile(pairs, first):
     lane, row = iota((8, 128), 1), iota((8, 128), 0)
     total = jnp.zeros((8, 128), F32)
-    for k, (a, b) in enumerate(pairs):
+    for k, (a, b) in enumerate(pairs, first):
         one = jnp.sum(jnp.sum(by_row(a * b), axis=0), axis=1, keepdims=True)
         at = ((lane == k) & (row < EACH)) | ((lane == 6 + k) & (row >= EACH) & (row < 6))
         total = jnp.where(at, one, total)
-    return jnp.sum(total, axis=0, keepdims=True)
+    return total
 
 
 def steps(row, p):
@@ -376,7 +376,7 @@
            src_v, mass_v, nb_v, ns_v, fl_v, s8_v, small_v, wide_v, inv_v,
            r_v, m_v, l_v, choose_v, e0_v, flip_v, x_v, g_v, xh_v, xl_v, first_v,
            stga0, stga1, bufa0, bufa1, stgb0, stgb1, bufb0, bufb1, st3a, st3b, buf3a, buf3b,
-           nat_v, stgm, bufm, y_v, edge_v, own_v, insem, ssem, rsem, opensem):
+           nat_v, stgm, bufm, y_v, edge_v, own_v, dots_v, insem, ssem, rsem, opensem, farsem):
     t = lax.axis_index("tile")
     lev = lax.axis_index("lev")
     plane, q = t // PLANE, t % PLANE
@@ -392,7 +392,9 @@
     xy_peers = [(dy, 0, dx, 0) for dy in (4, 3, 5, 2, 6, 1, 7, 0) for dx in (2, 1, 3, 0) if dy or dx]
     zc_peers = [(0, dz, 0, dl) for dz in (3, 2, 1, 0) for dl in range(LEVS) if dz or dl]
     l_peers = [(0, 0, 0, dl) for dl in (2, 3, 4, 5, 1)]
-    everyone = a_peers + b_peers + l_peers
+    far_peers = [(0, 1, 2, 0), (0, 3, 2, 0)]
+    between = [(0, 1, 0, 0), (0, 3, 0, 0)]
+    everyone = a_peers + l_peers + [peer for peer in b_peers if peer not in far_peers]
 
     moves = [(src_hbm.at[p, n], src_v.at[pl.ds(p * EACH + n, 1)]) for p in range(2) for n in range(EACH)]
     moves += [(mass_hbm, mass_v), (s8_hbm, s8_v), (small_hbm, small_v), (inv_hbm, inv_v),
@@ -455,6 +457,8 @@
     bufa0[plane] = tile
     pl.semaphore_wait(barrier, len(everyone))
     send(a_peers, lambda peer: stga0, bufa0.at[plane], 0)
+    for peer in between:
+        pl.semaphore_signal(farsem, 1, device_id=at(*peer), device_id_type=pl.DeviceIdType.MESH)
 
     polys = polynomial()[2]
     rhos = [polys]
@@ -477,6 +481,7 @@
         x_v[...] = newton(x_v[...], g_v[...], rhos[0], False)[0]
 
     done(a_peers, bufa0, 0, True)
+    pl.semaphore_wait(farsem, len(between))
     total = jnp.sum(bufa0[...], axis=0)[6:8]
     stgm[...] = total
     bufm[q] = total
@@ -527,6 +532,7 @@
     @pl.when(ready)
     def _():
         l_v[...] = local_field(x1, c)
+        dots_v[...] = dots_tile(((r, z0), (z0, q0)), 0)
 
     done(a_peers, bufa1, 2, True)
     stgb1[...] = tiles_b(bufa1[...], choose_v[...])
@@ -538,7 +544,8 @@
     edges, own = coarse_parts(y_v[...], s0, s1)
     w, v = finish(q0, l_v[...], mass, jnp.sum(bufb1[...], axis=0), flip, edges, own, c)
 
-    row = dots_row(((r, z0), (z0, q0), (r, w), (q0, w), (z0, v), (w, v)))
+    tile = dots_v[...] + dots_tile(((r, w), (q0, w), (z0, v), (w, v)), 2)
+    row = jnp.sum(tile, axis=0, keepdims=True)
     st3a[...] = row
     buf3a[plane * LINE + x_at] = row
     send(xy_peers, lambda peer: st3a, buf3a.at[plane * LINE + x_at], 4)
@@ -593,9 +600,9 @@
         one, one, column, column, plane, plane, plane, plane, line, line,
         pltpu.VMEM((COLUMN * LINE, 1, 128), F32), pltpu.VMEM((LINE * LEVS, 1, 128), F32),
         pltpu.VMEM((4, 8, SIDE * SIDE), F32),
-        pltpu.VMEM((2, 128), F32), pltpu.VMEM((PLANE, 2, 128), F32), pltpu.VMEM((40, SUBS), F32), one, one,
+        pltpu.VMEM((2, 128), F32), pltpu.VMEM((PLANE, 2, 128), F32), pltpu.VMEM((40, SUBS), F32), one, one, one,
         pltpu.SemaphoreType.DMA((14,)),
-        pltpu.SemaphoreType.DMA((7,)), pltpu.SemaphoreType.DMA((7,)), pltpu.SemaphoreType.REGULAR,
+        pltpu.SemaphoreType.DMA((7,)), pltpu.SemaphoreType.DMA((7,)), pltpu.SemaphoreType.REGULAR, pltpu.SemaphoreType.REGULAR,
     ]
     out = pltpu.VMEM((2,) + rows.shape, F32)
     both = pl.pallas_call(

time: 56 us -> 55.8 us (level)
  no operation moved by 1% of the time
where the time goes in v6:
time: 55.8 us; the launch traced here: 55.7 us
  Pallas kernels  54.4 us (97%)
  between operations  0.64 us (1%)
  local copies, waits for them, and re-layouts  0.62 us (1%)
    pallas_call x1, Pallas kernels, shards(): pl.pallas_call(kernel, out_shape=out, in_specs=[hbm] * len(args), out_spe...  54.4 us

profile of v6, /device:TPU:1, one launch (start us, length us, event | category | flops | bytes accessed | tf_op | source)
XLA Modules:
  0.0 55.7 jit_solution(13596588722597373087)
XLA Ops:
  0.6 54.4 %schwarz.1 = f32[2,2,3,1,1024]{4,3,2,1,0:T(1,128)S(1)} custom-call(f32[2,3,1,1024]{3,2,1,0:T(1,128)} %bitcast.8, f32[3,1024]{1,0:T(4,128)} %mass_hbm.1, s32[4,384]{1,0:T(4,128)} %bitcast.9, s32[4,384]{1,0:T(4,128)} %bitcast.10, s32[4,384]{1,0:T(4,128)} %bitcast.11, bf16[512,256]{1,0:T(8,128)(2,1)} %constant.8.clone.s8_hbm, ...), custom_call_target="tpu_custom_call" | custom-call | tf_op jit(solution)/shard_map/schwarz/pallas_call | solution.py:608
  55.0 0.6 %slice_bitcast_fusion = (f32[2,1,3,1024]{3,1,2,0:T(1,128)}, f32[2,1,3,1024]{3,1,2,0:T(1,128)}) fusion(f32[2,2,3,1,1024]{4,3,2,1,0:T(1,128)S(1)} %schwarz.1), kind=kLoop, calls=%fused_computation | loop fusion | bytes 98304 | tf_op jit(solution)/shard_map/squeeze | solution.py:618

commit v7 on v6

--- a/solution.py
+++ b/solution.py
@@ -261,8 +261,10 @@
 
 
 def newton(x, g, rho, last):
-    xs = split(x, 3)
-    gx = dot(g, xs[0]) + (dot(g, xs[1]) + dot(g, xs[2]))
+    xs = split(x, 3 if last else 2)
+    gx = dot(g, xs[0]) + dot(g, xs[1])
+    if last:
+        gx = gx + dot(g, xs[2])
     ones = (SIGMA / SUBS) * jnp.sum(x, axis=0, keepdims=True)
     eye = (iota((SUBS, SUBS), 0) == iota((SUBS, SUBS), 1)).astype(F32)
     rest = eye - ((128.0 + SHIFT) * x - 32.0 * gx + ones)

time: 55.8 us -> 55.8 us (level)
  no operation moved by 1% of the time
where the time goes in v7:
time: 55.8 us; the launch traced here: 55.7 us
  Pallas kernels  54.4 us (97%)
  between operations  0.64 us (1%)
  local copies, waits for them, and re-layouts  0.62 us (1%)
    pallas_call x1, Pallas kernels, shards(): pl.pallas_call(kernel, out_shape=out, in_specs=[hbm] * len(args), out_spe...  54.4 us

profile of v7, /device:TPU:1, one launch (start us, length us, event | category | flops | bytes accessed | tf_op | source)
XLA Modules:
  0.0 55.7 jit_solution(4633825549345686352)
XLA Ops:
  0.6 54.4 %schwarz.1 = f32[2,2,3,1,1024]{4,3,2,1,0:T(1,128)S(1)} custom-call(f32[2,3,1,1024]{3,2,1,0:T(1,128)} %bitcast.8, f32[3,1024]{1,0:T(4,128)} %mass_hbm.1, s32[4,384]{1,0:T(4,128)} %bitcast.9, s32[4,384]{1,0:T(4,128)} %bitcast.10, s32[4,384]{1,0:T(4,128)} %bitcast.11, bf16[512,256]{1,0:T(8,128)(2,1)} %constant.8.clone.s8_hbm, ...), custom_call_target="tpu_custom_call" | custom-call | tf_op jit(solution)/shard_map/schwarz/pallas_call | solution.py:610
  55.0 0.6 %slice_bitcast_fusion = (f32[2,1,3,1024]{3,1,2,0:T(1,128)}, f32[2,1,3,1024]{3,1,2,0:T(1,128)}) fusion(f32[2,2,3,1,1024]{4,3,2,1,0:T(1,128)S(1)} %schwarz.1), kind=kLoop, calls=%fused_computation | loop fusion | bytes 98304 | tf_op jit(solution)/shard_map/squeeze | solution.py:620

commit v8 on v7

--- a/solution.py
+++ b/solution.py
@@ -374,6 +374,10 @@
     return a0 + a1 * (1.0 + beta), a1 * a0
 
 
+def stack_rows(tiles):
+    return jnp.concatenate([jnp.sum(tiles, axis=0), jnp.zeros((2, 128), F32)], axis=0)
+
+
 def kernel(src_hbm, mass_hbm, nb_hbm, ns_hbm, fl_hbm, s8_hbm, small_hbm, wide_hbm, inv_hbm, out_ref,
            src_v, mass_v, nb_v, ns_v, fl_v, s8_v, small_v, wide_v, inv_v,
            r_v, m_v, l_v, choose_v, e0_v, flip_v, x_v, g_v, xh_v, xl_v, first_v,
@@ -490,7 +494,7 @@
     send(b_peers, lambda peer: stgm, bufm.at[q], 6)
     stgb0[...] = tiles_b(bufa0[...], choose_v[...])
     bufb0[q] = stgb0[q]
-    send(b_peers, lambda peer: stgb0.at[spot(peer)], bufb0.at[q], 1)
+    send(b_peers, lambda peer: stgb0.at[spot(peer), pl.ds(0, 6)], bufb0.at[q, pl.ds(0, 6)], 1)
 
     @pl.when(ready)
     def _():
@@ -516,13 +520,11 @@
         y_v[...] = y
         edge_v[...], own_v[...] = coarse_parts(y, s0, s1)
 
-    done(b_peers, bufb0, 1, True)
-    for peer in l_peers:
-        pl.semaphore_signal(opensem, 1, device_id=at(*peer), device_id_type=pl.DeviceIdType.MESH)
+    done(b_peers, bufb0.at[:, pl.ds(0, 6)], 1, True)
     c = consts()
     flip = flip_v[...]
     r, mass = r_v[...], m_v[...]
-    z0, q0 = finish(r, l_v[...], mass, jnp.sum(bufb0[...], axis=0), flip, edge_v[...], own_v[...], c)
+    z0, q0 = finish(r, l_v[...], mass, stack_rows(bufb0[:, 0:6, :]), flip, edge_v[...], own_v[...], c)
 
     x1 = coefficients(q0, c)
     rims = local_rims(x1, c)
@@ -530,6 +532,8 @@
     stga1[...] = tile
     bufa1[plane] = tile
     send(a_peers, lambda peer: stga1, bufa1.at[plane], 2)
+    for peer in l_peers:
+        pl.semaphore_signal(opensem, 1, device_id=at(*peer), device_id_type=pl.DeviceIdType.MESH)
 
     @pl.when(ready)
     def _():
@@ -577,7 +581,7 @@
                 out_ref[k, p, n] = out[p * EACH + n : p * EACH + n + 1]
 
     done(a_peers, bufa0, 0, False)
-    done(b_peers, bufb0, 1, False)
+    done(b_peers, bufb0.at[:, pl.ds(0, 6)], 1, False)
     done(a_peers, bufa1, 2, False)
     done(b_peers, bufb1, 3, False)
     done(xy_peers, buf3a, 4, False)

time: 55.8 us -> 55.8 us (level)
  no operation moved by 1% of the time
where the time goes in v8:
time: 55.8 us; the launch traced here: 55.7 us
  Pallas kernels  54.4 us (97%)
  between operations  0.64 us (1%)
  local copies, waits for them, and re-layouts  0.62 us (1%)
    pallas_call x1, Pallas kernels, shards(): pl.pallas_call(kernel, out_shape=out, in_specs=[hbm] * len(args), out_spe...  54.4 us

profile of v8, /device:TPU:1, one launch (start us, length us, event | category | flops | bytes accessed | tf_op | source)
XLA Modules:
  0.0 55.7 jit_solution(14683539062066582305)
XLA Ops:
  0.6 54.4 %schwarz.1 = f32[2,2,3,1,1024]{4,3,2,1,0:T(1,128)S(1)} custom-call(f32[2,3,1,1024]{3,2,1,0:T(1,128)} %bitcast.8, f32[3,1024]{1,0:T(4,128)} %mass_hbm.1, s32[4,384]{1,0:T(4,128)} %bitcast.9, s32[4,384]{1,0:T(4,128)} %bitcast.10, s32[4,384]{1,0:T(4,128)} %bitcast.11, bf16[512,256]{1,0:T(8,128)(2,1)} %constant.8.clone.s8_hbm, ...), custom_call_target="tpu_custom_call" | custom-call | tf_op jit(solution)/shard_map/schwarz/pallas_call | solution.py:614
  55.0 0.6 %slice_bitcast_fusion = (f32[2,1,3,1024]{3,1,2,0:T(1,128)}, f32[2,1,3,1024]{3,1,2,0:T(1,128)}) fusion(f32[2,2,3,1,1024]{4,3,2,1,0:T(1,128)S(1)} %schwarz.1), kind=kLoop, calls=%fused_computation | loop fusion | bytes 98304 | tf_op jit(solution)/shard_map/squeeze | solution.py:624

commit v9 on v8

--- a/solution.py
+++ b/solution.py
@@ -531,7 +531,7 @@
     tile = tile_a(rims, packed(q0, plane), zrow)
     stga1[...] = tile
     bufa1[plane] = tile
-    send(a_peers, lambda peer: stga1, bufa1.at[plane], 2)
+    send(a_peers, lambda peer: stga1.at[pl.ds(0, 7)], bufa1.at[plane, pl.ds(0, 7)], 2)
     for peer in l_peers:
         pl.semaphore_signal(opensem, 1, device_id=at(*peer), device_id_type=pl.DeviceIdType.MESH)
 
@@ -540,15 +540,15 @@
         l_v[...] = local_field(x1, c)
         dots_v[...] = dots_tile(((r, z0), (z0, q0)), 0)
 
-    done(a_peers, bufa1, 2, True)
-    stgb1[...] = tiles_b(bufa1[...], choose_v[...])
+    done(a_peers, bufa1.at[:, pl.ds(0, 7)], 2, True)
+    stgb1[...] = tiles_b(jnp.where(iota((COLUMN, 8, 128), 1) < 7, bufa1[...], 0.0), choose_v[...])
     bufb1[q] = stgb1[q]
-    send(b_peers, lambda peer: stgb1.at[spot(peer)], bufb1.at[q], 3)
-    done(b_peers, bufb1, 3, True)
+    send(b_peers, lambda peer: stgb1.at[spot(peer), pl.ds(0, 7)], bufb1.at[q, pl.ds(0, 7)], 3)
+    done(b_peers, bufb1.at[:, pl.ds(0, 7)], 3, True)
     sums = bufb1[:, 6, :]
     s0, s1 = to_vectors(jnp.concatenate([sums, roll(sums, 128 - EACH, 1)], axis=0), c)
     edges, own = coarse_parts(y_v[...], s0, s1)
-    w, v = finish(q0, l_v[...], mass, jnp.sum(bufb1[...], axis=0), flip, edges, own, c)
+    w, v = finish(q0, l_v[...], mass, stack_rows(bufb1[:, 0:6, :]), flip, edges, own, c)
 
     tile = dots_v[...] + dots_tile(((r, w), (q0, w), (z0, v), (w, v)), 2)
     row = jnp.sum(tile, axis=0, keepdims=True)
@@ -582,8 +582,8 @@
 
     done(a_peers, bufa0, 0, False)
     done(b_peers, bufb0.at[:, pl.ds(0, 6)], 1, False)
-    done(a_peers, bufa1, 2, False)
-    done(b_peers, bufb1, 3, False)
+    done(a_peers, bufa1.at[:, pl.ds(0, 7)], 2, False)
+    done(b_peers, bufb1.at[:, pl.ds(0, 7)], 3, False)
     done(xy_peers, buf3a, 4, False)
     done(zc_peers, buf3b, 5, False)
     done(b_peers, bufm, 6, False)

time: 55.8 us -> 55.8 us (level)
  no operation moved by 1% of the time
where the time goes in v9:
time: 55.8 us; the launch traced here: 55.6 us
  Pallas kernels  54.4 us (97%)
  between operations  0.64 us (1%)
  local copies, waits for them, and re-layouts  0.62 us (1%)
    pallas_call x1, Pallas kernels, shards(): pl.pallas_call(kernel, out_shape=out, in_specs=[hbm] * len(args), out_spe...  54.4 us

profile of v9, /device:TPU:1, one launch (start us, length us, event | category | flops | bytes accessed | tf_op | source)
XLA Modules:
  0.0 55.6 jit_solution(10751346736281381570)
XLA Ops:
  0.6 54.4 %schwarz.1 = f32[2,2,3,1,1024]{4,3,2,1,0:T(1,128)S(1)} custom-call(f32[2,3,1,1024]{3,2,1,0:T(1,128)} %bitcast.8, f32[3,1024]{1,0:T(4,128)} %mass_hbm.1, s32[4,384]{1,0:T(4,128)} %bitcast.9, s32[4,384]{1,0:T(4,128)} %bitcast.10, s32[4,384]{1,0:T(4,128)} %bitcast.11, bf16[512,256]{1,0:T(8,128)(2,1)} %constant.8.clone.s8_hbm, ...), custom_call_target="tpu_custom_call" | custom-call | tf_op jit(solution)/shard_map/schwarz/pallas_call | solution.py:614
  55.0 0.6 %slice_bitcast_fusion = (f32[2,1,3,1024]{3,1,2,0:T(1,128)}, f32[2,1,3,1024]{3,1,2,0:T(1,128)}) fusion(f32[2,2,3,1,1024]{4,3,2,1,0:T(1,128)S(1)} %schwarz.1), kind=kLoop, calls=%fused_computation | loop fusion | bytes 98304 | tf_op jit(solution)/shard_map/squeeze | solution.py:624
